TPU v7x, 32 devices: a whole 2x2x4 slice. The times are simulated.
32 devices in a mesh: grp: 4 (over z), inner: 8 (over y, x, core).
Axes of the slice: x: 2, y: 2, z: 4, core: 2. Of those that a mesh axis runs over, the one named last changes fastest.
Arguments:
- design: float32 [8, 4096, 1024], P('inner', 'grp'), may hold values from -6 to 6
- row_signs: int32 [8, 4096], P('inner', 'grp'), may hold values from 0 to 1
- kept_rows: int32 [8, 2048], P('inner'), may hold values from 0 to 4095, as said below
Outputs:
- factored: float32 [2048, 1024], P('grp')
Inputs may be any that keep to these rules, and one draw needn't show every extreme that they name: `kept_rows`: within each block the 2048 kept row numbers are distinct, and each block keeps its first and its last row.
All inputs are finite; a program needn't handle non-finite values.
Results may differ from a plain program's by a relative error of at most 0.0048.
Values may be sent and summed in bfloat16 or wider, within the bound.
No kernel may reach another device: no remote copies, remote signals or barrier semaphores. Data moves between devices by JAX's collectives and lax.ppermute only.
A program may use at most 64 MiB of HBM per device.

v0:
```python
import math

import jax
import jax.numpy as jnp
from jax import lax
from jax.sharding import PartitionSpec as P

COLS_DONE = 8


epsilon = 1e-06


def sign_table(row_ids, col_ids):
    common_bits = jnp.bitwise_and(row_ids[:, None], col_ids[None, :])
    ones_total = jnp.zeros(common_bits.shape, jnp.int32)
    for bit_pos in range(4):
        ones_total = ones_total + jnp.bitwise_and(jnp.right_shift(common_bits, bit_pos), 1)
    return 1.0 - 2.0 * jnp.bitwise_and(ones_total, 1).astype(jnp.float32)


def pick_rows(table_rows, chosen_rows):
    return jnp.take(table_rows, chosen_rows, axis=0)


def on_device(design, row_signs, kept_rows):
    block_count, local_rows, columns = design.shape
    keep_count = kept_rows.shape[1]
    groups = lax.axis_size("grp")
    owned_rows = keep_count // groups
    highest = lax.Precision.HIGHEST
    sixteen = jnp.arange(16, dtype=jnp.int32)
    hadamard = sign_table(sixteen, sixteen).astype(jnp.bfloat16)
    flipped = (design * (1 - 2 * row_signs).astype(jnp.float32)[:, :, None]).astype(jnp.bfloat16)
    lowest = flipped.reshape(block_count * local_rows // 16, 16, columns)
    first_pass = jnp.einsum(
        "hc,ncd->nhd", hadamard, lowest, preferred_element_type=jnp.float32
    ).astype(jnp.bfloat16)
    middle_view = first_pass.reshape(block_count * local_rows // 256, 16, 16, columns)
    second_pass = jnp.einsum(
        "hb,mbcd->mhcd", hadamard, middle_view, preferred_element_type=jnp.float32
    ).astype(jnp.bfloat16)
    second_pass = second_pass.reshape(block_count, local_rows, columns)
    gathered_rows = lax.all_to_all(second_pass, "grp", split_axis=2, concat_axis=1, tiled=True)
    col_count = gathered_rows.shape[2]
    by_piece = gathered_rows.reshape(block_count, 16, 256, col_count)
    mixed_rows = jnp.einsum("ha,nakd->nhkd", hadamard, by_piece, preferred_element_type=jnp.float32)
    mixed_rows = mixed_rows.reshape(block_count, 16 * 256, col_count)
    picked = jax.vmap(pick_rows)(mixed_rows, kept_rows)
    partial_value = jnp.sum(picked, axis=0)
    summed = lax.psum(partial_value, "inner")
    sketch = lax.all_to_all(summed, "grp", split_axis=0, concat_axis=1, tiled=True)
    sketch = sketch * (1.0 / (64.0 * math.sqrt(keep_count)))
    row_base = lax.axis_index("grp") * owned_rows
    global_rows = row_base + jnp.arange(owned_rows, dtype=jnp.int32)

    def reflect(col_index, current):
        column = jnp.where(global_rows >= col_index, current[:, col_index], 0.0)
        is_pivot = (global_rows == col_index).astype(jnp.float32)
        norm_sq, crossed, pivot_row = lax.psum(
            (
                jnp.sum(column * column),
                jnp.dot(column, current, precision=highest),
                jnp.dot(is_pivot, current, precision=highest),
            ),
            "grp",
        )
        pivot_value = pivot_row[col_index]
        head_value = -jnp.where(pivot_value >= 0, 1.0, -1.0) * jnp.sqrt(norm_sq)
        length = 2.0 * (norm_sq - head_value * pivot_value) + epsilon
        projected_row = crossed - head_value * pivot_row
        vector = column - head_value * is_pivot
        return current - vector[:, None] * (2.0 * projected_row / length)[None, :]

    result = lax.fori_loop(0, COLS_DONE, reflect, sketch)
    return result


def solution(mesh):
    return jax.shard_map(
        on_device,
        mesh=mesh,
        in_specs=(P("inner", "grp", None), P("inner", "grp"), P("inner", None)),
        out_specs=P("grp", None),
        check_vma=False,
    )
```

profile of v0, /device:TPU:0, one launch (start us, length us, event | category | flops | bytes accessed | tf_op | source)
XLA Modules:
  0.0 397.2 jit_solution(10092679646443896874)
XLA Ops:
  7.2 2.5 multiply_convert_fusion
  13.1 7.7 %copy.22 = bf16[1,1024,1024]{1,0,2:T(2,128)(2,1)} copy(bf16[1,1024,1024]{2,1,0:T(8,128)(2,1)S(1)} %bitcast.77) | data formatting | bytes 4194304 | tf_op jit(solution)/shard_map/reshape | solution.py:43
  21.4 12.8 %reduce.2 = bf16[1024,1024]{1,0:T(8,128)(2,1)S(1)} reduce(bf16[1024,1,1024]{2,1,0:T(2,128)(2,1)} %bitcast.75, bf16[]{:T(256)} %broadcast.106), dimensions={1}, to_apply=%bitcast.43.reduce_sub_computation | reduce | bytes 4194306
  34.2 2.8 reshape.93
  36.9 6.5 %all-to-all-start = ((bf16[4,2,131072]{2,1,0:T(2,128)(2,1)}), bf16[4,2,131072]{2,1,0:T(2,128)(2,1)S(1)}, u32[]{:S(2)}, u32[]{:S(2)}) async-start(bf16[4,2,131072]{2,1,0:T(2,128)(2,1)} %reshape.93), calls=%async_computation | async-start | bytes 4194304 | tf_op jit(solution)/shard_map/all_to_all | solution.py:44
  43.5 48.1 %all-to-all-done = bf16[4,2,131072]{2,1,0:T(2,128)(2,1)S(1)} async-done(((bf16[4,2,131072]{2,1,0:T(2,128)(2,1)}), bf16[4,2,131072]{2,1,0:T(2,128)(2,1)S(1)}, u32[]{:S(2)}, u32[]{:S(2)}) %all-to-all-start) | async-done | bytes 2097184 | tf_op jit(solution)/shard_map/all_to_all | solution.py:44
  91.6 3.4 reshape.94
  94.9 3.0 copy.29
  97.9 2.6 copy.23
  100.5 2.9 convolution_bitcast_fusion
  103.4 4.4 %copy.25 = f32[1,16,256,256]{3,2,1,0:T(8,128)} copy(f32[1,16,256,256]{3,1,2,0:T(8,128)S(1)} %convolution_bitcast_fusion) | data formatting | bytes 8388608 | tf_op jit(solution)/shard_map/ha,nakd->nhkd/transpose | solution.py:47
  107.8 21.4 %gather_fusion = f32[2048,256]{1,0:T(8,128)S(1)} fusion(f32[1,4096,256]{2,1,0:T(8,128)} %bitcast.74, s32[2048]{0:T(1024)S(1)} %bitcast.73), kind=kCustom, calls=%fused_computation | custom fusion | bytes 4210688 | tf_op jit(solution)/shard_map/vmap(jit(_take))/gather | solution.py:23
  130.9 61.0 %all-reduce.5.cloned.1.call-done = f32[4,512,256]{2,1,0:T(8,128)} async-done(((f32[4,512,256]{2,1,0:T(8,128)}), f32[4,512,256]{2,1,0:T(8,128)}) %all-reduce.5.cloned.1.call-update) | async-done | bytes 2097168 | tf_op jit(solution)/shard_map/psum | solution.py:51
  191.9 4.5 %all-to-all-start.1 = ((f32[4,512,256]{2,1,0:T(8,128)}), f32[4,512,256]{2,1,0:T(8,128)S(1)}, u32[]{:S(2)}, u32[]{:S(2)}) async-start(f32[4,512,256]{2,1,0:T(8,128)} %all-reduce.5.cloned.1.call-done), calls=%async_computation.1 | async-start | bytes 4194304 | tf_op jit(solution)/shard_map/all_to_all | solution.py:52
  196.4 47.1 %all-to-all-done.1 = f32[4,512,256]{2,1,0:T(8,128)S(1)} async-done(((f32[4,512,256]{2,1,0:T(8,128)}), f32[4,512,256]{2,1,0:T(8,128)S(1)}, u32[]{:S(2)}, u32[]{:S(2)}) %all-to-all-start.1) | async-done | bytes 2097184 | tf_op jit(solution)/shard_map/all_to_all | solution.py:52
  245.0 1.9 copy.26
  247.0 141.5 %while.14 = (s32[]{:T(128)}, f32[512,1024]{0,1:T(8,128)S(1)}, s32[]{:T(128)}, s32[]{:T(128)}, f32[]{:T(128)}, /*index=5*/f32[]{:T(128)}, f32[]{:T(128)}, f32[]{:T(128)}, f32[]{:T(128)}) while((s32[]{:T(128)}, f32[512,1024]{0,1:T(8,128)S(1)}, s32[]{:T(128)}, s32[]{:T(128)}, f32[]{:T(128)}, /*index=5*/f32[]{:T(128)}, f32[]{:T(128)}, ...), condition=%wide.region_6.7_spmd.clone, body=%wide.region_1.6_spmd.clone.sunk | while | flops 13643786 | bytes 8453379 | solution.py:75
  247.6 1.8 fusion.55
  250.5 10.8 %all-reduce.2 = (f32[1024]{0:T(1024)S(1)}, f32[1024]{0:T(1024)S(1)}, f32[]{:T(128)}) all-reduce(f32[1024]{0:T(1024)S(1)} %bitcast.83, f32[1024]{0:T(1024)S(1)} %bitcast.84, f32[]{:T(128)} %get-tuple-element.117), channel_id=1, replica_groups=mesh['grp'=4,'inner'=8] {'grp'}, use_global_device_ids=true, to_apply=%region_5.5 | all-reduce | flops 2049 | bytes 16392 | tf_op jit(solution)/shard_map/while/body/eval_jaxpr/psum | solution.py:60
  265.8 1.8 fusion.55
  268.6 9.9 %all-reduce.2 = (f32[1024]{0:T(1024)S(1)}, f32[1024]{0:T(1024)S(1)}, f32[]{:T(128)}) all-reduce(f32[1024]{0:T(1024)S(1)} %bitcast.83, f32[1024]{0:T(1024)S(1)} %bitcast.84, f32[]{:T(128)} %get-tuple-element.117), channel_id=1, replica_groups=mesh['grp'=4,'inner'=8] {'grp'}, use_global_device_ids=true, to_apply=%region_5.5 | all-reduce | flops 2049 | bytes 16392 | tf_op jit(solution)/shard_map/while/body/eval_jaxpr/psum | solution.py:60
  283.0 1.8 fusion.55
  285.9 10.8 %all-reduce.2 = (f32[1024]{0:T(1024)S(1)}, f32[1024]{0:T(1024)S(1)}, f32[]{:T(128)}) all-reduce(f32[1024]{0:T(1024)S(1)} %bitcast.83, f32[1024]{0:T(1024)S(1)} %bitcast.84, f32[]{:T(128)} %get-tuple-element.117), channel_id=1, replica_groups=mesh['grp'=4,'inner'=8] {'grp'}, use_global_device_ids=true, to_apply=%region_5.5 | all-reduce | flops 2049 | bytes 16392 | tf_op jit(solution)/shard_map/while/body/eval_jaxpr/psum | solution.py:60
  301.1 1.8 fusion.55
  304.0 9.9 %all-reduce.2 = (f32[1024]{0:T(1024)S(1)}, f32[1024]{0:T(1024)S(1)}, f32[]{:T(128)}) all-reduce(f32[1024]{0:T(1024)S(1)} %bitcast.83, f32[1024]{0:T(1024)S(1)} %bitcast.84, f32[]{:T(128)} %get-tuple-element.117), channel_id=1, replica_groups=mesh['grp'=4,'inner'=8] {'grp'}, use_global_device_ids=true, to_apply=%region_5.5 | all-reduce | flops 2049 | bytes 16392 | tf_op jit(solution)/shard_map/while/body/eval_jaxpr/psum | solution.py:60
  318.4 1.8 fusion.55
  321.3 10.8 %all-reduce.2 = (f32[1024]{0:T(1024)S(1)}, f32[1024]{0:T(1024)S(1)}, f32[]{:T(128)}) all-reduce(f32[1024]{0:T(1024)S(1)} %bitcast.83, f32[1024]{0:T(1024)S(1)} %bitcast.84, f32[]{:T(128)} %get-tuple-element.117), channel_id=1, replica_groups=mesh['grp'=4,'inner'=8] {'grp'}, use_global_device_ids=true, to_apply=%region_5.5 | all-reduce | flops 2049 | bytes 16392 | tf_op jit(solution)/shard_map/while/body/eval_jaxpr/psum | solution.py:60
  336.5 1.8 fusion.55
  339.4 9.9 %all-reduce.2 = (f32[1024]{0:T(1024)S(1)}, f32[1024]{0:T(1024)S(1)}, f32[]{:T(128)}) all-reduce(f32[1024]{0:T(1024)S(1)} %bitcast.83, f32[1024]{0:T(1024)S(1)} %bitcast.84, f32[]{:T(128)} %get-tuple-element.117), channel_id=1, replica_groups=mesh['grp'=4,'inner'=8] {'grp'}, use_global_device_ids=true, to_apply=%region_5.5 | all-reduce | flops 2049 | bytes 16392 | tf_op jit(solution)/shard_map/while/body/eval_jaxpr/psum | solution.py:60
  356.6 10.8 %all-reduce.2 = (f32[1024]{0:T(1024)S(1)}, f32[1024]{0:T(1024)S(1)}, f32[]{:T(128)}) all-reduce(f32[1024]{0:T(1024)S(1)} %bitcast.83, f32[1024]{0:T(1024)S(1)} %bitcast.84, f32[]{:T(128)} %get-tuple-element.117), channel_id=1, replica_groups=mesh['grp'=4,'inner'=8] {'grp'}, use_global_device_ids=true, to_apply=%region_5.5 | all-reduce | flops 2049 | bytes 16392 | tf_op jit(solution)/shard_map/while/body/eval_jaxpr/psum | solution.py:60
  374.8 9.9 %all-reduce.2 = (f32[1024]{0:T(1024)S(1)}, f32[1024]{0:T(1024)S(1)}, f32[]{:T(128)}) all-reduce(f32[1024]{0:T(1024)S(1)} %bitcast.83, f32[1024]{0:T(1024)S(1)} %bitcast.84, f32[]{:T(128)} %get-tuple-element.117), channel_id=1, replica_groups=mesh['grp'=4,'inner'=8] {'grp'}, use_global_device_ids=true, to_apply=%region_5.5 | all-reduce | flops 2049 | bytes 16392 | tf_op jit(solution)/shard_map/while/body/eval_jaxpr/psum | solution.py:60
  388.5 1.8 copy.27
  (97 shorter events, 33.5 us)
Async XLA Ops:
  36.9 6.5 %copy-start = (s32[1,2048]{1,0:T(1,128)S(1)}, s32[1,2048]{1,0:T(1,128)}, u32[]{:S(2)}) copy-start(s32[1,2048]{1,0:T(1,128)} %param.7) | copy-start | bytes 24580
  36.9 54.7 %all-to-all-start = ((bf16[4,2,131072]{2,1,0:T(2,128)(2,1)}), bf16[4,2,131072]{2,1,0:T(2,128)(2,1)S(1)}, u32[]{:S(2)}, u32[]{:S(2)}) async-start(bf16[4,2,131072]{2,1,0:T(2,128)(2,1)} %reshape.93), calls=%async_computation | async-start | bytes 4194304 | tf_op jit(solution)/shard_map/all_to_all | solution.py:44
  43.4 148.5 %all-reduce.5.cloned.1.call-start = ((), (), s32[]{:S(2)}) async-start(), calls=%async_computation.2 | async-start | bytes 4194304 | tf_op jit(solution)/shard_map/psum | solution.py:51
  191.9 51.6 %all-to-all-start.1 = ((f32[4,512,256]{2,1,0:T(8,128)}), f32[4,512,256]{2,1,0:T(8,128)S(1)}, u32[]{:S(2)}, u32[]{:S(2)}) async-start(f32[4,512,256]{2,1,0:T(8,128)} %all-reduce.5.cloned.1.call-done), calls=%async_computation.1 | async-start | bytes 4194304 | tf_op jit(solution)/shard_map/all_to_all | solution.py:52
Sparse Core Ops, SparseCore 0:
  131.0 60.8 all-reduce.4
where the time goes:
time: 398 us; the launch traced here: 397 us
  waiting for transfers between devices  156 us (39%)
  blocking collectives  82.7 us (21%)
  local copies, waits for them, and re-layouts  56 us (14%)
  matrix products  28 us (7%)
  other arithmetic  27.4 us (7%)
  loops' own time  22.4 us (6%)
  between operations  13.5 us (3%)
  starting transfers between devices  11 us (3%)
    psum x8, blocking collectives, reflect(): lax.psum((jnp.sum(column * column), jnp.dot(column, current, precision=hi...  82.7 us
    psum x1, waiting for transfers between devices, on_device(): summed = lax.psum(partial_value, 'inner')  61 us
    all_to_all x1, waiting for transfers between devices, on_device(): lax.all_to_all(second_pass, 'grp', split_axis=2, concat_axis=1, tiled=True)  48.1 us
    all_to_all x1, waiting for transfers between devices, on_device(): lax.all_to_all(summed, 'grp', split_axis=0, concat_axis=1, tiled=True)  47.1 us
    another operation x1, loops' own time, on_device(): result = lax.fori_loop(0, COLS_DONE, reflect, sketch)  22.4 us
    gather x2, local copies, waits for them, and re-layouts, pick_rows(): return jnp.take(table_rows, chosen_rows, axis=0)  21.4 us
    dot_general x8, matrix products, reflect(): jnp.dot(column, current, precision=highest)  14.5 us
    unnamed x1, other arithmetic  12.8 us
  transfers between devices with their start and end apart: 3, of which 3 were waited for; matrix products, arithmetic and copies ran while one was open for 0% of the time, Pallas kernels for 0%

commit v1 on v0

--- a/solution.py
+++ b/solution.py
@@ -1,12 +1,16 @@
+import functools
 import math
 
 import jax
 import jax.numpy as jnp
 from jax import lax
+from jax.experimental import pallas as pl
+from jax.experimental.pallas import tpu as pltpu
 from jax.sharding import PartitionSpec as P
 
 COLS_DONE = 8
-
+LANES = 128
+LOW = 256
 
 epsilon = 1e-06
 
@@ -23,7 +27,7 @@
     return jnp.take(table_rows, chosen_rows, axis=0)
 
 
-def on_device(design, row_signs, kept_rows):
+def plain_form(design, row_signs, kept_rows):
     block_count, local_rows, columns = design.shape
     keep_count = kept_rows.shape[1]
     groups = lax.axis_size("grp")
@@ -72,11 +76,330 @@
         vector = column - head_value * is_pivot
         return current - vector[:, None] * (2.0 * projected_row / length)[None, :]
 
-    result = lax.fori_loop(0, COLS_DONE, reflect, sketch)
-    return result
+    return lax.fori_loop(0, COLS_DONE, reflect, sketch)
+
+
+def swap(value, axis, mask):
+    pairs = [(place, place ^ mask) for place in range(lax.axis_size(axis))]
+    return lax.ppermute(value, axis, pairs)
+
+
+def odd_ones(bits):
+    bits = bits ^ (bits >> 2)
+    bits = bits ^ (bits >> 1)
+    return bits & 1
+
+
+def low_hadamard(shift):
+    row = lax.broadcasted_iota(jnp.int32, (LOW, LOW), 0)
+    col = lax.broadcasted_iota(jnp.int32, (LOW, LOW), 1)
+    signs = 1 - 2 * odd_ones((row & col) >> shift & 15)
+    same = ((row ^ col) & (255 - (15 << shift))) == 0
+    return jnp.where(same, signs, 0).astype(jnp.float32)
+
+
+def passes(signs_ref, data_refs, mixed_ref):
+    inner_table = low_hadamard(0)
+    outer_table = low_hadamard(4).astype(jnp.bfloat16)
+    for piece in range(mixed_ref.shape[0] // LOW):
+        rows = pl.ds(piece * LOW, LOW)
+        flips = (1 - 2 * signs_ref[:, rows]).astype(jnp.float32)
+        table = (inner_table * flips).astype(jnp.bfloat16)
+        data = jnp.concatenate([ref[rows, :].astype(jnp.bfloat16) for ref in data_refs], axis=1)
+        first = jnp.dot(table, data, preferred_element_type=jnp.float32).astype(jnp.bfloat16)
+        second = jnp.dot(outer_table, first, preferred_element_type=jnp.float32)
+        mixed_ref[rows, :] = second.astype(jnp.bfloat16)
+
+
+def choice(kept_ref, first_piece, pieces):
+    kept = jnp.broadcast_to(kept_ref[...], (8, kept_ref.shape[1]))
+    line = lax.broadcasted_iota(jnp.int32, kept.shape, 0)
+    signs = 1 - 2 * odd_ones((kept >> 8) & (first_piece + line))
+    packed = jnp.where(line < pieces, signs, kept & 255).astype(jnp.float32)
+    tall = packed.T
+    lane = lax.broadcasted_iota(jnp.int32, (kept.shape[1], LOW), 1).astype(jnp.float32)
+    hit = tall[:, pieces : pieces + 1] == lane
+    parts = [jnp.where(hit, tall[:, piece : piece + 1], 0.0).astype(jnp.bfloat16) for piece in range(pieces)]
+    return jnp.concatenate(parts, axis=1)
+
+
+def contribution_kernel(pieces, place_ref, kept_ref, signs_ref, *refs):
+    *data_refs, out_ref, mixed_ref = refs
+
+    @pl.when(pl.program_id(0) == 0)
+    def _():
+        passes(signs_ref, data_refs, mixed_ref)
+
+    table = choice(kept_ref, place_ref[1] * pieces, pieces)
+    part = jnp.dot(table, mixed_ref[...], preferred_element_type=jnp.float32)
+    width = data_refs[0].shape[1]
+    for index in range(len(data_refs)):
+        out_ref[index] = part[:, index * width : (index + 1) * width].astype(out_ref.dtype)
+
+
+def contribution(place, kept, signs, data, width, masks, dtype, steps=4):
+    rows, keep = data.shape[0], kept.shape[1]
+    tall = keep // steps
+
+    def column_group(mask):
+        return pl.BlockSpec((rows, width), lambda s, place_ref: (0, place_ref[0] ^ mask))
+
+    return pl.pallas_call(
+        functools.partial(contribution_kernel, rows // LOW),
+        out_shape=jax.ShapeDtypeStruct((len(masks), keep, width), dtype),
+        grid_spec=pltpu.PrefetchScalarGridSpec(
+            num_scalar_prefetch=1,
+            grid=(steps,),
+            in_specs=[
+                pl.BlockSpec((1, tall), lambda s, place_ref: (0, s)),
+                pl.BlockSpec((1, rows), lambda s, place_ref: (0, 0)),
+            ]
+            + [column_group(mask) for mask in masks],
+            out_specs=pl.BlockSpec((len(masks), tall, width), lambda s, place_ref: (0, s, 0)),
+            scratch_shapes=[pltpu.VMEM((rows, len(masks) * width), jnp.bfloat16)],
+        ),
+        name="contribution",
+    )(place, kept, signs, *([data] * len(masks)))
+
+
+def panel_kernel(pieces, place_ref, kept_ref, signs_ref, data_ref, out_ref, mixed_ref):
+    @pl.when(pl.program_id(0) == 0)
+    def _():
+        passes(signs_ref, [data_ref], mixed_ref)
+
+    table = choice(kept_ref, place_ref[1] * pieces, pieces)
+    part = jnp.dot(table, mixed_ref[...], preferred_element_type=jnp.float32)
+    out_ref[...] = part.T[:COLS_DONE, :]
+
+
+def panel_contribution(place, kept, signs, data, steps=4):
+    rows, keep = data.shape[0], kept.shape[1]
+    tall = keep // steps
+    return pl.pallas_call(
+        functools.partial(panel_kernel, rows // LOW),
+        out_shape=jax.ShapeDtypeStruct((COLS_DONE, keep), jnp.float32),
+        grid_spec=pltpu.PrefetchScalarGridSpec(
+            num_scalar_prefetch=1,
+            grid=(steps,),
+            in_specs=[
+                pl.BlockSpec((1, tall), lambda s, place_ref: (0, s)),
+                pl.BlockSpec((1, rows), lambda s, place_ref: (0, 0)),
+                pl.BlockSpec((rows, LANES), lambda s, place_ref: (0, 0)),
+            ],
+            out_specs=pl.BlockSpec((COLS_DONE, tall), lambda s, place_ref: (0, s)),
+            scratch_shapes=[pltpu.VMEM((rows, LANES), jnp.bfloat16)],
+        ),
+        name="panel",
+    )(place, kept, signs, data)
+
+
+def factor_kernel(scale, panel_ref, vectors_ref, weights_ref):
+    current = panel_ref[...] * scale
+    count, keep = current.shape
+    lane = lax.broadcasted_iota(jnp.int32, (1, keep), 1)
+    line = lax.broadcasted_iota(jnp.int32, (count, 1), 0)
+    short = lax.broadcasted_iota(jnp.int32, (1, LANES), 1)
+    vectors = jnp.zeros((count, keep), jnp.float32)
+    weights = jnp.zeros((count, LANES), jnp.float32)
+    for j in range(count):
+        column = jnp.where(lane >= j, current[j : j + 1, :], 0.0)
+        is_pivot = lane == j
+        crossed = jnp.sum(current * column, axis=1, keepdims=True)
+        pivot_row = jnp.sum(jnp.where(is_pivot, current, 0.0), axis=1, keepdims=True)
+        norm_sq = crossed[j : j + 1, :]
+        pivot = pivot_row[j : j + 1, :]
+        head = jnp.where(pivot >= 0, -1.0, 1.0) * jnp.sqrt(norm_sq)
+        length = 2.0 * (norm_sq - head * pivot) + epsilon
+        vector = column - jnp.where(is_pivot, head, 0.0)
+        projected = crossed - head * pivot_row
+        current = current - (2.0 * projected / length) * vector
+        shared = jnp.sum(vectors * vector, axis=1, keepdims=True)
+        unit = jnp.where(short == j, 1.0, 0.0)
+        row = (2.0 / length) * (unit - jnp.sum(shared * weights, axis=0, keepdims=True))
+        vectors = jnp.where(line == j, vector, vectors)
+        weights = jnp.where(line == j, row, weights)
+    vectors_ref[...] = vectors
+    weights_ref[...] = weights
+
+
+def factor(panel, scale):
+    count, keep = panel.shape
+    return pl.pallas_call(
+        functools.partial(factor_kernel, scale),
+        out_shape=(
+            jax.ShapeDtypeStruct((count, keep), jnp.float32),
+            jax.ShapeDtypeStruct((count, LANES), jnp.float32),
+        ),
+        name="factor",
+    )(panel)
+
+
+def split_two(value):
+    high = value.astype(jnp.bfloat16)
+    low = (value - high.astype(jnp.float32)).astype(jnp.bfloat16)
+    return jnp.concatenate([high, low], axis=0)
+
+
+def spread_kernel(scale, arrived_count, place_ref, vectors_ref, base_ref, *refs):
+    arrived, outs = refs[:arrived_count], refs[arrived_count:]
+    *send_refs, own_ref, product_ref = outs
+    rows = own_ref.shape[0]
+    count = vectors_ref.shape[0]
+
+    def total(window):
+        value = base_ref[window, :]
+        for ref in arrived:
+            value = value + ref[window, :].astype(jnp.float32)
+        return value * scale
+
+    whole = total(slice(None)).astype(jnp.bfloat16)
+    both = jnp.dot(split_two(vectors_ref[...]), whole, preferred_element_type=jnp.float32)
+    product = both[:count] + both[count:]
+    product_ref[...] = product
+    pair = split_two(product)
+
+    def window_of(mask):
+        return pl.ds(pl.multiple_of((place_ref[1] ^ mask) * rows, rows), rows)
+
+    own_ref[...] = total(window_of(0))
+    for index, send_ref in enumerate(send_refs):
+        send_ref[:rows, :] = total(window_of(index + 1)).astype(jnp.bfloat16)
+        send_ref[rows:, :] = pair
+
+
+def spread(place, vectors, base, arrived, groups, scale):
+    keep, width = base.shape
+    count = vectors.shape[0]
+    rows = keep // groups
+    vmem = pl.BlockSpec(memory_space=pltpu.VMEM)
+    outs = [jax.ShapeDtypeStruct((rows + 2 * count, width), jnp.bfloat16)] * (groups - 1)
+    outs += [jax.ShapeDtypeStruct((rows, width), jnp.float32), jax.ShapeDtypeStruct((count, width), jnp.float32)]
+    return pl.pallas_call(
+        functools.partial(spread_kernel, scale, len(arrived)),
+        out_shape=tuple(outs),
+        in_specs=[pl.BlockSpec(memory_space=pltpu.SMEM)] + [vmem] * (2 + len(arrived)),
+        out_specs=(vmem,) * len(outs),
+        name="spread",
+    )(place, vectors, base, *arrived)
+
+
+def apply_kernel(place_ref, vectors_ref, weights_ref, own_ref, product_ref, *refs):
+    *arrived, out_ref = refs
+    rows = own_ref.shape[0]
+    count = vectors_ref.shape[0]
+    value = own_ref[...]
+    product = product_ref[...]
+    for ref in arrived:
+        value = value + ref[:rows, :].astype(jnp.float32)
+        pair = ref[rows:, :].astype(jnp.float32)
+        product = product + (pair[:count] + pair[count:])
+    highest = lax.Precision.HIGHEST
+    multipliers = jnp.dot(
+        weights_ref[:, :count], product, precision=highest, preferred_element_type=jnp.float32
+    )
+    window = pl.ds(pl.multiple_of(place_ref[1] * rows, rows), rows)
+    vectors = vectors_ref[:, window]
+    update = lax.dot_general(
+        vectors, multipliers, (((0,), (0,)), ((), ())), precision=highest, preferred_element_type=jnp.float32
+    )
+    out_ref[...] = (value - update).astype(jnp.bfloat16)
+
+
+def apply(place, vectors, weights, own, product, arrived):
+    vmem = pl.BlockSpec(memory_space=pltpu.VMEM)
+    return pl.pallas_call(
+        apply_kernel,
+        out_shape=jax.ShapeDtypeStruct(own.shape, jnp.bfloat16),
+        in_specs=[pl.BlockSpec(memory_space=pltpu.SMEM)] + [vmem] * (4 + len(arrived)),
+        out_specs=vmem,
+        name="apply",
+    )(place, vectors, weights, own, product, *arrived)
+
+
+def lay_kernel(masks, place_ref, *refs):
+    *parts, out_ref = refs
+    width = parts[0].shape[1]
+    for mask, ref in zip(masks, parts):
+        start = pl.multiple_of((place_ref[0] ^ mask) * width, width)
+        out_ref[:, pl.ds(start, width)] = ref[...].astype(jnp.float32)
+
+
+def lay(place, parts, masks):
+    rows, width = parts[0].shape
+    vmem = pl.BlockSpec(memory_space=pltpu.VMEM)
+    return pl.pallas_call(
+        functools.partial(lay_kernel, masks),
+        out_shape=jax.ShapeDtypeStruct((rows, width * len(parts)), jnp.float32),
+        in_specs=[pl.BlockSpec(memory_space=pltpu.SMEM)] + [vmem] * len(parts),
+        out_specs=vmem,
+        name="lay",
+    )(place, *parts)
+
+
+def wide_form(design, row_signs, kept_rows):
+    data = design[0]
+    columns = data.shape[1]
+    keep = kept_rows.shape[1]
+    groups, members = lax.axis_size("grp"), lax.axis_size("inner")
+    width = columns // members
+    scale = 1.0 / (64.0 * math.sqrt(keep))
+    place = jnp.stack([lax.axis_index("inner"), lax.axis_index("grp")]).astype(jnp.int32)
+    make = functools.partial(contribution, place, kept_rows, row_signs, data, width)
+    far = list(range(2, members, 2))
+    order = far + [0]
+    sums = {}
+    for start in range(0, len(order), 2):
+        pair = order[start : start + 2]
+        sent = make([mask ^ 1 for mask in pair], jnp.bfloat16)
+        arrived = swap(sent, "inner", 1)
+        own = make(pair, jnp.float32)
+        for index, mask in enumerate(pair):
+            sums[mask] = own[index] + arrived[index].astype(jnp.float32)
+    moved = [swap(sums[mask].astype(jnp.bfloat16), "inner", mask) for mask in far]
+
+    panel = panel_contribution(place, kept_rows, row_signs, data)
+    for axis, size in (("inner", members), ("grp", groups)):
+        mask = 1
+        while mask < size:
+            panel = panel + swap(panel, axis, mask)
+            mask *= 2
+    vectors, weights = factor(panel, scale)
+
+    *sends, own, product = spread(place, vectors, sums[0], moved, groups, scale)
+    got = [swap(value, "grp", index + 1) for index, value in enumerate(sends)]
+    done = apply(place, vectors, weights, own, product, got)
+    parts = [done] + [swap(done, "inner", mask) for mask in far]
+    masks = [0] + far
+    parts += [swap(part, "inner", 1) for part in parts]
+    masks += [mask ^ 1 for mask in masks]
+    return lay(place, parts, masks)
+
+
+def power_of_two(size):
+    return size & (size - 1) == 0
 
 
 def solution(mesh):
+    groups, members = mesh.shape["grp"], mesh.shape["inner"]
+
+    def on_device(design, row_signs, kept_rows):
+        block_count, local_rows, columns = design.shape
+        keep = kept_rows.shape[1]
+        fits = (
+            block_count == 1
+            and power_of_two(groups)
+            and power_of_two(members)
+            and members >= 4
+            and groups >= 2
+            and columns % (members * LANES) == 0
+            and local_rows % LOW == 0
+            and local_rows // LOW < 8
+            and keep % (groups * LANES) == 0
+            and keep % 512 == 0
+        )
+        form = wide_form if fits else plain_form
+        return form(design, row_signs, kept_rows)
+
     return jax.shard_map(
         on_device,
         mesh=mesh,

time: 398 us -> 108 us (0.27)
  waiting for transfers between devices: 156 us -> 36.8 us
  blocking collectives: 82.7 us -> 0 us
  local copies, waits for them, and re-layouts: 56 us -> 2.46 us
  Pallas kernels: 0 us -> 41.7 us
  matrix products: 28 us -> 0 us
  loops' own time: 22.4 us -> 0 us
  other arithmetic: 27.4 us -> 5.8 us
  between operations: 13.5 us -> 0.14 us
  starting transfers between devices: 11 us -> 20.4 us
    all_to_all x2 -> x0, waiting for transfers between devices: 95.2 us -> none  [the longest x1 48.1 us: on_device(): lax.all_to_all(second_pass, 'grp', split_axis=2, concat_axis=1, tiled=True)]
    psum x8 -> x0, blocking collectives: 82.7 us -> none  [reflect(): lax.psum((jnp.sum(column * column), jnp.dot(column, current, precision=hi...]
    psum x1 -> x0, waiting for transfers between devices: 61 us -> none  [on_device(): summed = lax.psum(partial_value, 'inner')]
    pallas_call x0 -> x9, Pallas kernels: none -> 41.7 us  [the longest x4 25.1 us: contribution(): pl.pallas_call(functools.partial(contribution_kernel, rows // LOW), out_s...]
    ppermute x0 -> x20, waiting for transfers between devices: none -> 36.8 us  [swap(): return lax.ppermute(value, axis, pairs)]
    dot_general x19 -> x0, matrix products: 28 us -> none  [the longest x8 14.5 us: reflect(): jnp.dot(column, current, precision=highest)]
    another operation x1 -> x0, loops' own time: 22.4 us -> none  [on_device(): result = lax.fori_loop(0, COLS_DONE, reflect, sketch)]
    gather x2 -> x0, local copies, waits for them, and re-layouts: 21.4 us -> none  [pick_rows(): return jnp.take(table_rows, chosen_rows, axis=0)]
  transfers between devices with their start and end apart: 3 -> 20, of which waited for: 3 -> 13; matrix products, arithmetic and copies ran while one was open for 0% -> 5% of each run, Pallas kernels for 0% -> 25%
where the time goes in v1:
time: 108 us; the launch traced here: 107 us
  Pallas kernels  41.7 us (39%)
  waiting for transfers between devices  36.8 us (34%)
  starting transfers between devices  20.4 us (19%)
  other arithmetic  5.8 us (5%)
  local copies, waits for them, and re-layouts  2.46 us (2%)
    ppermute x20, waiting for transfers between devices, swap(): return lax.ppermute(value, axis, pairs)  36.8 us
    pallas_call x4, Pallas kernels, contribution(): pl.pallas_call(functools.partial(contribution_kernel, rows // LOW), out_s...  25.1 us
    ppermute x20, starting transfers between devices, swap(): return lax.ppermute(value, axis, pairs)  20.4 us
    pallas_call x1, Pallas kernels, panel_contribution(): pl.pallas_call(functools.partial(panel_kernel, rows // LOW), out_shape=ja...  5.97 us
    convert_element_type x2, other arithmetic, wide_form(): sums[mask].astype(jnp.bfloat16)  3.72 us
    pallas_call x1, Pallas kernels, spread(): pl.pallas_call(functools.partial(spread_kernel, scale, len(arrived)), out...  2.99 us
    pallas_call x1, Pallas kernels, lay(): pl.pallas_call(functools.partial(lay_kernel, masks), out_shape=jax.ShapeD...  2.88 us
    unnamed x30, local copies, waits for them, and re-layouts  2.46 us
  transfers between devices with their start and end apart: 20, of which 13 were waited for; matrix products, arithmetic and copies ran while one was open for 5% of the time, Pallas kernels for 25%

profile of v1, /device:TPU:0, one launch (start us, length us, event | category | flops | bytes accessed | tf_op | source)
XLA Modules:
  0.0 107.3 jit_solution(1436712809261631033)
XLA Ops:
  0.6 6.2 %contribution.7 = bf16[2,2048,128]{2,1,0:T(8,128)(2,1)} custom-call(s32[2]{0:T(128)} %pad_add_fusion.place_ref, s32[1,2048]{1,0:T(1,128)} %kept_ref.9, s32[1,1024]{1,0:T(1,128)} %signs_ref.9, f32[1024,1024]{1,0:T(8,128)} %bitcast.11, f32[1024,1024]{1,0:T(8,128)} %bitcast.12), custom_call_target="tpu_custom_call" | custom-call | tf_op jit(solution)/shard_map/contribution/pallas_call | solution.py:147
  7.3 6.2 %contribution.5 = bf16[2,2048,128]{2,1,0:T(8,128)(2,1)} custom-call(s32[2]{0:T(128)} %pad_add_fusion.place_ref, s32[1,2048]{1,0:T(1,128)} %kept_ref.9, s32[1,1024]{1,0:T(1,128)} %signs_ref.9, f32[1024,1024]{1,0:T(8,128)} %bitcast.13, f32[1024,1024]{1,0:T(8,128)} %bitcast.14), custom_call_target="tpu_custom_call" | custom-call | tf_op jit(solution)/shard_map/contribution/pallas_call | solution.py:147
  13.5 6.3 %contribution.6 = f32[2,2048,128]{2,1,0:T(8,128)} custom-call(s32[2]{0:T(128)} %pad_add_fusion.place_ref, s32[1,2048]{1,0:T(1,128)} %kept_ref.9, s32[1,1024]{1,0:T(1,128)} %signs_ref.9, f32[1024,1024]{1,0:T(8,128)} %bitcast.15, f32[1024,1024]{1,0:T(8,128)} %bitcast.16), custom_call_target="tpu_custom_call" | custom-call | tf_op jit(solution)/shard_map/contribution/pallas_call | solution.py:147
  19.8 6.4 %contribution.4 = f32[2,2048,128]{2,1,0:T(8,128)} custom-call(s32[2]{0:T(128)} %pad_add_fusion.place_ref, s32[1,2048]{1,0:T(1,128)} %kept_ref.9, s32[1,1024]{1,0:T(1,128)} %signs_ref.9, f32[1024,1024]{1,0:T(8,128)} %bitcast.17, f32[1024,1024]{1,0:T(8,128)} %bitcast.18), custom_call_target="tpu_custom_call" | custom-call | tf_op jit(solution)/shard_map/contribution/pallas_call | solution.py:147
  26.2 2.5 %fusion.5 = (bf16[2048,128]{1,0:T(8,128)(2,1)}, bf16[2048,128]{1,0:T(8,128)(2,1)}) fusion(f32[2,2048,128]{2,1,0:T(8,128)S(1)} %copy-done.1, bf16[2,2048,128]{2,1,0:T(8,128)(2,1)} %collective-permute-done.6), kind=kLoop, calls=%fused_computation.9 | loop fusion | flops 1572864 | bytes 4194304 | tf_op jit(solution)/shard_map/convert_element_type | solution.py:358
  28.7 3.0 %collective-permute-start.8 = (bf16[2048,128]{1,0:T(8,128)(2,1)}, bf16[2048,128]{1,0:T(8,128)(2,1)S(1)}, u32[]{:S(2)}, u32[]{:S(2)}) collective-permute-start(bf16[2048,128]{1,0:T(8,128)(2,1)} %get-tuple-element.21), channel_id=1, source_target_pairs={{0,4},{1,5},{2,6},{3,7},{4,0},{5,1},{6,2},{7,3},{8,12},{9,13},{10,... | collective-permute-start | bytes 1572872 | tf_op jit(solution)/shard_map/ppermute | solution.py:84
  31.7 1.5 %collective-permute-start.7 = (bf16[2048,128]{1,0:T(8,128)(2,1)}, bf16[2048,128]{1,0:T(8,128)(2,1)S(1)}, u32[]{:S(2)}, u32[]{:S(2)}) collective-permute-start(bf16[2048,128]{1,0:T(8,128)(2,1)} %get-tuple-element.22), channel_id=1, source_target_pairs={{0,2},{1,3},{2,0},{3,1},{4,6},{5,7},{6,4},{7,5},{8,10},{9,11},{10,... | collective-permute-start | bytes 1572872 | tf_op jit(solution)/shard_map/ppermute | solution.py:84
  33.2 1.2 %fusion.6 = (bf16[2048,128]{1,0:T(8,128)(2,1)S(1)}, f32[2048,128]{1,0:T(8,128)}) fusion(f32[2,2048,128]{2,1,0:T(8,128)S(1)} %copy-done, bf16[2,2048,128]{2,1,0:T(8,128)(2,1)S(1)} %collective-permute-done.5), kind=kLoop, calls=%fused_computation.10 | loop fusion | flops 1310720 | bytes 4718592 | tf_op jit(solution)/shard_map/convert_element_type | solution.py:358
  34.4 6.0 %panel.1 = f32[8,2048]{1,0:T(8,128)} custom-call(s32[2]{0:T(128)} %pad_add_fusion.place_ref, s32[1,2048]{1,0:T(1,128)} %kept_ref.9, s32[1,1024]{1,0:T(1,128)} %signs_ref.9, f32[1024,1024]{1,0:T(8,128)} %bitcast.19), custom_call_target="tpu_custom_call" | custom-call | tf_op jit(solution)/shard_map/panel/pallas_call | solution.py:178
  40.4 1.5 %collective-permute-done = f32[8,2048]{1,0:T(8,128)S(1)} collective-permute-done((f32[8,2048]{1,0:T(8,128)}, f32[8,2048]{1,0:T(8,128)S(1)}, u32[]{:S(2)}, u32[]{:S(2)}) %collective-permute-start) | collective-permute-done | bytes 65568 | tf_op jit(solution)/shard_map/ppermute | solution.py:84
  41.8 0.9 add.32
  42.7 2.0 %collective-permute-start.1 = (f32[8,2048]{1,0:T(8,128)S(1)}, f32[8,2048]{1,0:T(8,128)S(1)}, u32[]{:S(2)}, u32[]{:S(2)}) collective-permute-start(f32[8,2048]{1,0:T(8,128)S(1)} %add.32), channel_id=1, source_target_pairs={{0,2},{1,3},{2,0},{3,1},{4,6},{5,7},{6,4},{7,5},{8,10},{9,11},{10,... | collective-permute-start | bytes 196616 | tf_op jit(solution)/shard_map/ppermute | solution.py:84
  44.7 13.4 %collective-permute-done.1 = f32[8,2048]{1,0:T(8,128)S(1)} collective-permute-done((f32[8,2048]{1,0:T(8,128)S(1)}, f32[8,2048]{1,0:T(8,128)S(1)}, u32[]{:S(2)}, u32[]{:S(2)}) %collective-permute-start.1) | collective-permute-done | bytes 65568 | tf_op jit(solution)/shard_map/ppermute | solution.py:84
  58.5 4.0 %collective-permute-done.2 = f32[8,2048]{1,0:T(8,128)S(1)} collective-permute-done((f32[8,2048]{1,0:T(8,128)S(1)}, f32[8,2048]{1,0:T(8,128)S(1)}, u32[]{:S(2)}, u32[]{:S(2)}) %collective-permute-start.2) | collective-permute-done | bytes 65568 | tf_op jit(solution)/shard_map/ppermute | solution.py:84
  62.5 1.6 %collective-permute-start.3 = (f32[8,2048]{1,0:T(8,128)S(1)}, f32[8,2048]{1,0:T(8,128)S(1)}, u32[]{:S(2)}, u32[]{:S(2)}) collective-permute-start(f32[8,2048]{1,0:T(8,128)S(1)} %add.34), channel_id=1, source_target_pairs={{0,8},{8,0},{16,24},{24,16},{1,9},{9,1},{17,25},{25,17},{2,10},{10... | collective-permute-start | bytes 196616 | tf_op jit(solution)/shard_map/ppermute | solution.py:84
  64.1 2.7 %collective-permute-done.3 = f32[8,2048]{1,0:T(8,128)S(1)} collective-permute-done((f32[8,2048]{1,0:T(8,128)S(1)}, f32[8,2048]{1,0:T(8,128)S(1)}, u32[]{:S(2)}, u32[]{:S(2)}) %collective-permute-start.3) | collective-permute-done | bytes 65568 | tf_op jit(solution)/shard_map/ppermute | solution.py:84
  66.8 3.2 %collective-permute-start.4 = (f32[8,2048]{1,0:T(8,128)S(1)}, f32[8,2048]{1,0:T(8,128)S(1)}, u32[]{:S(2)}, u32[]{:S(2)}) collective-permute-start(f32[8,2048]{1,0:T(8,128)S(1)} %add.35), channel_id=1, source_target_pairs={{0,16},{8,24},{16,0},{24,8},{1,17},{9,25},{17,1},{25,9},{2,18},{10... | collective-permute-start | bytes 196616 | tf_op jit(solution)/shard_map/ppermute | solution.py:84
  70.0 2.2 %collective-permute-done.4 = f32[8,2048]{1,0:T(8,128)S(1)} collective-permute-done((f32[8,2048]{1,0:T(8,128)S(1)}, f32[8,2048]{1,0:T(8,128)S(1)}, u32[]{:S(2)}, u32[]{:S(2)}) %collective-permute-start.4) | collective-permute-done | bytes 65568 | tf_op jit(solution)/shard_map/ppermute | solution.py:84
  72.9 2.5 %factor.1 = (f32[8,2048]{1,0:T(8,128)}, f32[8,128]{1,0:T(8,128)}) custom-call(f32[8,2048]{1,0:T(8,128)} %add.36.panel_ref), custom_call_target="tpu_custom_call" | custom-call | tf_op jit(solution)/shard_map/factor/pallas_call | solution.py:227
  75.4 0.8 copy-done.2
  76.5 3.0 %spread.1 = (bf16[528,128]{1,0:T(8,128)(2,1)}, bf16[528,128]{1,0:T(8,128)(2,1)}, bf16[528,128]{1,0:T(8,128)(2,1)}, f32[512,128]{1,0:T(8,128)}, f32[8,128]{1,0:T(8,128)}) custom-call(s32[2]{0:T(128)} %pad_add_fusion.place_ref, f32[8,2048]{1,0:T(8,128)} %get-tuple-element.12.vectors_ref, f32[2048,128]{1,0:T(8,128)} %get-tuple-element.20.base_ref, ...), custom_call_target="tpu_custom_call" | custom-call | tf_op jit(solution)/shard_map/spread/pallas_call | solution.py:277
  79.5 1.4 %collective-permute-start.10 = (bf16[528,128]{1,0:T(8,128)(2,1)}, bf16[528,128]{1,0:T(8,128)(2,1)S(1)}, u32[]{:S(2)}, u32[]{:S(2)}) collective-permute-start(bf16[528,128]{1,0:T(8,128)(2,1)} %get-tuple-element.16), channel_id=1, source_target_pairs={{0,8},{8,0},{16,24},{24,16},{1,9},{9,1},{17,25},{25,17},{2,10},{10... | collective-permute-start | bytes 405512 | tf_op jit(solution)/shard_map/ppermute | solution.py:84
  80.9 3.3 %collective-permute-start.11 = (bf16[528,128]{1,0:T(8,128)(2,1)}, bf16[528,128]{1,0:T(8,128)(2,1)S(1)}, u32[]{:S(2)}, u32[]{:S(2)}) collective-permute-start(bf16[528,128]{1,0:T(8,128)(2,1)} %get-tuple-element.17), channel_id=1, source_target_pairs={{0,16},{8,24},{16,0},{24,8},{1,17},{9,25},{17,1},{25,9},{2,18},{10... | collective-permute-start | bytes 405512 | tf_op jit(solution)/shard_map/ppermute | solution.py:84
  84.2 3.2 %collective-permute-done.10.refs_0_ = bf16[528,128]{1,0:T(8,128)(2,1)S(1)} collective-permute-done((bf16[528,128]{1,0:T(8,128)(2,1)}, bf16[528,128]{1,0:T(8,128)(2,1)S(1)}, u32[]{:S(2)}, u32[]{:S(2)}) %collective-permute-start.10) | collective-permute-done | bytes 135200 | tf_op jit(solution)/shard_map/ppermute | solution.py:84
  87.4 1.6 %collective-permute-done.11.refs_1_ = bf16[528,128]{1,0:T(8,128)(2,1)S(1)} collective-permute-done((bf16[528,128]{1,0:T(8,128)(2,1)}, bf16[528,128]{1,0:T(8,128)(2,1)S(1)}, u32[]{:S(2)}, u32[]{:S(2)}) %collective-permute-start.11) | collective-permute-done | bytes 135200 | tf_op jit(solution)/shard_map/ppermute | solution.py:84
  89.0 2.3 %collective-permute-done.12.refs_2_ = bf16[528,128]{1,0:T(8,128)(2,1)S(1)} collective-permute-done((bf16[528,128]{1,0:T(8,128)(2,1)}, bf16[528,128]{1,0:T(8,128)(2,1)S(1)}, u32[]{:S(2)}, u32[]{:S(2)}) %collective-permute-start.12) | collective-permute-done | bytes 135200 | tf_op jit(solution)/shard_map/ppermute | solution.py:84
  91.9 2.3 %apply.1.refs_0_ = bf16[512,128]{1,0:T(8,128)(2,1)} custom-call(s32[2]{0:T(128)} %pad_add_fusion.place_ref, f32[8,2048]{1,0:T(8,128)} %get-tuple-element.12.vectors_ref, f32[8,128]{1,0:T(8,128)} %get-tuple-element.13.weights_ref, f32[512,128]{1,0:T(8,128)} %get-tuple-element.14.own_ref, f32[8,128]{1,0:T(8,128)} %get-tuple-element.15.product_ref, ...), custom_call_target="tpu_custom_call" | custom-call | tf_op jit(solution)/shard_map/apply/pallas_call | solution.py:310
  94.3 1.4 %collective-permute-start.15 = (bf16[512,128]{1,0:T(8,128)(2,1)}, bf16[512,128]{1,0:T(8,128)(2,1)S(1)}, u32[]{:S(2)}, u32[]{:S(2)}) collective-permute-start(bf16[512,128]{1,0:T(8,128)(2,1)} %apply.1.refs_0_), channel_id=1, source_target_pairs={{0,6},{1,7},{2,4},{3,5},{4,2},{5,3},{6,0},{7,1},{8,14},{9,15},{10,... | collective-permute-start | bytes 393224 | tf_op jit(solution)/shard_map/ppermute | solution.py:84
  95.7 1.5 %collective-permute-start.14 = (bf16[512,128]{1,0:T(8,128)(2,1)}, bf16[512,128]{1,0:T(8,128)(2,1)S(1)}, u32[]{:S(2)}, u32[]{:S(2)}) collective-permute-start(bf16[512,128]{1,0:T(8,128)(2,1)} %apply.1.refs_0_), channel_id=1, source_target_pairs={{0,4},{1,5},{2,6},{3,7},{4,0},{5,1},{6,2},{7,3},{8,12},{9,13},{10,... | collective-permute-start | bytes 393224 | tf_op jit(solution)/shard_map/ppermute | solution.py:84
  97.8 2.7 %collective-permute-done.15.refs_3_ = bf16[512,128]{1,0:T(8,128)(2,1)S(1)} collective-permute-done((bf16[512,128]{1,0:T(8,128)(2,1)}, bf16[512,128]{1,0:T(8,128)(2,1)S(1)}, u32[]{:S(2)}, u32[]{:S(2)}) %collective-permute-start.15) | collective-permute-done | bytes 131104 | tf_op jit(solution)/shard_map/ppermute | solution.py:84
  100.4 1.3 %collective-permute-done.14.refs_2_ = bf16[512,128]{1,0:T(8,128)(2,1)S(1)} collective-permute-done((bf16[512,128]{1,0:T(8,128)(2,1)}, bf16[512,128]{1,0:T(8,128)(2,1)S(1)}, u32[]{:S(2)}, u32[]{:S(2)}) %collective-permute-start.14) | collective-permute-done | bytes 131104 | tf_op jit(solution)/shard_map/ppermute | solution.py:84
  104.4 2.9 %lay.1 = f32[512,1024]{1,0:T(8,128)} custom-call(s32[2]{0:T(128)} %pad_add_fusion.place_ref, bf16[512,128]{1,0:T(8,128)(2,1)} %apply.1.refs_0_, bf16[512,128]{1,0:T(8,128)(2,1)} %copy-done.10, bf16[512,128]{1,0:T(8,128)(2,1)} %copy-done.9, bf16[512,128]{1,0:T(8,128)(2,1)} %copy-done.8, bf16[512,128]{1,0:T(8,128)(2,1)} %copy-done.11, ...), custom_call_target="tpu_custom_call" | custom-call | tf_op jit(solution)/shard_map/lay/pallas_call | solution.py:330
  (55 shorter events, 6.3 us)
Async XLA Ops:
  6.8 19.4 %collective-permute-start.6 = (bf16[2,2048,128]{2,1,0:T(8,128)(2,1)}, bf16[2,2048,128]{2,1,0:T(8,128)(2,1)}, u32[]{:S(2)}, u32[]{:S(2)}) collective-permute-start(bf16[2,2048,128]{2,1,0:T(8,128)(2,1)} %contribution.7), channel_id=1, source_target_pairs={{0,1},{1,0},{2,3},{3,2},{4,5},{5,4},{6,7},{7,6},{8,9},{9,8},{10,11... | collective-permute-start | bytes 3145736 | tf_op jit(solution)/shard_map/ppermute | solution.py:84
  13.5 19.8 %collective-permute-start.5 = (bf16[2,2048,128]{2,1,0:T(8,128)(2,1)}, bf16[2,2048,128]{2,1,0:T(8,128)(2,1)S(1)}, u32[]{:S(2)}, u32[]{:S(2)}) collective-permute-start(bf16[2,2048,128]{2,1,0:T(8,128)(2,1)} %contribution.5), channel_id=1, source_target_pairs={{0,1},{1,0},{2,3},{3,2},{4,5},{5,4},{6,7},{7,6},{8,9},{9,8},{10,11... | collective-permute-start | bytes 3145736 | tf_op jit(solution)/shard_map/ppermute | solution.py:84
  19.8 6.4 %copy-start.1 = (f32[2,2048,128]{2,1,0:T(8,128)S(1)}, f32[2,2048,128]{2,1,0:T(8,128)}, u32[]{:S(2)}) copy-start(f32[2,2048,128]{2,1,0:T(8,128)} %contribution.6) | copy-start | bytes 6291460
  26.2 7.0 %copy-start = (f32[2,2048,128]{2,1,0:T(8,128)S(1)}, f32[2,2048,128]{2,1,0:T(8,128)}, u32[]{:S(2)}) copy-start(f32[2,2048,128]{2,1,0:T(8,128)} %contribution.4) | copy-start | bytes 6291460
  28.7 46.6 %collective-permute-start.8 = (bf16[2048,128]{1,0:T(8,128)(2,1)}, bf16[2048,128]{1,0:T(8,128)(2,1)S(1)}, u32[]{:S(2)}, u32[]{:S(2)}) collective-permute-start(bf16[2048,128]{1,0:T(8,128)(2,1)} %get-tuple-element.21), channel_id=1, source_target_pairs={{0,4},{1,5},{2,6},{3,7},{4,0},{5,1},{6,2},{7,3},{8,12},{9,13},{10,... | collective-permute-start | bytes 1572872 | tf_op jit(solution)/shard_map/ppermute | solution.py:84
  31.7 43.6 %collective-permute-start.7 = (bf16[2048,128]{1,0:T(8,128)(2,1)}, bf16[2048,128]{1,0:T(8,128)(2,1)S(1)}, u32[]{:S(2)}, u32[]{:S(2)}) collective-permute-start(bf16[2048,128]{1,0:T(8,128)(2,1)} %get-tuple-element.22), channel_id=1, source_target_pairs={{0,2},{1,3},{2,0},{3,1},{4,6},{5,7},{6,4},{7,5},{8,10},{9,11},{10,... | collective-permute-start | bytes 1572872 | tf_op jit(solution)/shard_map/ppermute | solution.py:84
  34.4 41.0 %collective-permute-start.9 = (bf16[2048,128]{1,0:T(8,128)(2,1)S(1)}, bf16[2048,128]{1,0:T(8,128)(2,1)S(1)}, u32[]{:S(2)}, u32[]{:S(2)}) collective-permute-start(bf16[2048,128]{1,0:T(8,128)(2,1)S(1)} %get-tuple-element.19), channel_id=1, source_target_pairs={{0,6},{1,7},{2,4},{3,5},{4,2},{5,3},{6,0},{7,1},{8,14},{9,15},{10,... | collective-permute-start | bytes 1572872 | tf_op jit(solution)/shard_map/ppermute | solution.py:84
  40.4 1.5 %collective-permute-start = (f32[8,2048]{1,0:T(8,128)}, f32[8,2048]{1,0:T(8,128)S(1)}, u32[]{:S(2)}, u32[]{:S(2)}) collective-permute-start(f32[8,2048]{1,0:T(8,128)} %panel.1), channel_id=1, source_target_pairs={{0,1},{1,0},{2,3},{3,2},{4,5},{5,4},{6,7},{7,6},{8,9},{9,8},{10,11... | collective-permute-start | bytes 196616 | tf_op jit(solution)/shard_map/ppermute | solution.py:84
  42.7 15.4 %collective-permute-start.1 = (f32[8,2048]{1,0:T(8,128)S(1)}, f32[8,2048]{1,0:T(8,128)S(1)}, u32[]{:S(2)}, u32[]{:S(2)}) collective-permute-start(f32[8,2048]{1,0:T(8,128)S(1)} %add.32), channel_id=1, source_target_pairs={{0,2},{1,3},{2,0},{3,1},{4,6},{5,7},{6,4},{7,5},{8,10},{9,11},{10,... | collective-permute-start | bytes 196616 | tf_op jit(solution)/shard_map/ppermute | solution.py:84
  58.1 4.3 %collective-permute-start.2 = (f32[8,2048]{1,0:T(8,128)S(1)}, f32[8,2048]{1,0:T(8,128)S(1)}, u32[]{:S(2)}, u32[]{:S(2)}) collective-permute-start(f32[8,2048]{1,0:T(8,128)S(1)} %add.33), channel_id=1, source_target_pairs={{0,4},{1,5},{2,6},{3,7},{4,0},{5,1},{6,2},{7,3},{8,12},{9,13},{10,... | collective-permute-start | bytes 196616 | tf_op jit(solution)/shard_map/ppermute | solution.py:84
  62.5 4.3 %collective-permute-start.3 = (f32[8,2048]{1,0:T(8,128)S(1)}, f32[8,2048]{1,0:T(8,128)S(1)}, u32[]{:S(2)}, u32[]{:S(2)}) collective-permute-start(f32[8,2048]{1,0:T(8,128)S(1)} %add.34), channel_id=1, source_target_pairs={{0,8},{8,0},{16,24},{24,16},{1,9},{9,1},{17,25},{25,17},{2,10},{10... | collective-permute-start | bytes 196616 | tf_op jit(solution)/shard_map/ppermute | solution.py:84
  66.8 5.4 %collective-permute-start.4 = (f32[8,2048]{1,0:T(8,128)S(1)}, f32[8,2048]{1,0:T(8,128)S(1)}, u32[]{:S(2)}, u32[]{:S(2)}) collective-permute-start(f32[8,2048]{1,0:T(8,128)S(1)} %add.35), channel_id=1, source_target_pairs={{0,16},{8,24},{16,0},{24,8},{1,17},{9,25},{17,1},{25,9},{2,18},{10... | collective-permute-start | bytes 196616 | tf_op jit(solution)/shard_map/ppermute | solution.py:84
  75.3 0.8 copy-start.2
  75.3 1.0 copy-start.3
  75.4 1.1 %copy-start.4 = (bf16[2048,128]{1,0:T(8,128)(2,1)}, bf16[2048,128]{1,0:T(8,128)(2,1)S(1)}, u32[]{:S(2)}) copy-start(bf16[2048,128]{1,0:T(8,128)(2,1)S(1)} %collective-permute-done.9.refs_2_) | copy-start | bytes 1572868
  79.5 7.9 %collective-permute-start.10 = (bf16[528,128]{1,0:T(8,128)(2,1)}, bf16[528,128]{1,0:T(8,128)(2,1)S(1)}, u32[]{:S(2)}, u32[]{:S(2)}) collective-permute-start(bf16[528,128]{1,0:T(8,128)(2,1)} %get-tuple-element.16), channel_id=1, source_target_pairs={{0,8},{8,0},{16,24},{24,16},{1,9},{9,1},{17,25},{25,17},{2,10},{10... | collective-permute-start | bytes 405512 | tf_op jit(solution)/shard_map/ppermute | solution.py:84
  80.9 8.1 %collective-permute-start.11 = (bf16[528,128]{1,0:T(8,128)(2,1)}, bf16[528,128]{1,0:T(8,128)(2,1)S(1)}, u32[]{:S(2)}, u32[]{:S(2)}) collective-permute-start(bf16[528,128]{1,0:T(8,128)(2,1)} %get-tuple-element.17), channel_id=1, source_target_pairs={{0,16},{8,24},{16,0},{24,8},{1,17},{9,25},{17,1},{25,9},{2,18},{10... | collective-permute-start | bytes 405512 | tf_op jit(solution)/shard_map/ppermute | solution.py:84
  84.2 7.1 %collective-permute-start.12 = (bf16[528,128]{1,0:T(8,128)(2,1)}, bf16[528,128]{1,0:T(8,128)(2,1)S(1)}, u32[]{:S(2)}, u32[]{:S(2)}) collective-permute-start(bf16[528,128]{1,0:T(8,128)(2,1)} %get-tuple-element.18), channel_id=1, source_target_pairs={{0,24},{8,16},{16,8},{24,0},{1,25},{9,17},{17,9},{25,1},{2,26},{10... | collective-permute-start | bytes 405512 | tf_op jit(solution)/shard_map/ppermute | solution.py:84
  87.3 3.9 %copy-start.5 = (bf16[528,128]{1,0:T(8,128)(2,1)}, bf16[528,128]{1,0:T(8,128)(2,1)S(1)}, u32[]{:S(2)}) copy-start(bf16[528,128]{1,0:T(8,128)(2,1)S(1)} %collective-permute-done.10.refs_0_) | copy-start | bytes 405508
  89.0 2.3 %copy-start.6 = (bf16[528,128]{1,0:T(8,128)(2,1)}, bf16[528,128]{1,0:T(8,128)(2,1)S(1)}, u32[]{:S(2)}) copy-start(bf16[528,128]{1,0:T(8,128)(2,1)S(1)} %collective-permute-done.11.refs_1_) | copy-start | bytes 405508
  94.3 6.2 %collective-permute-start.15 = (bf16[512,128]{1,0:T(8,128)(2,1)}, bf16[512,128]{1,0:T(8,128)(2,1)S(1)}, u32[]{:S(2)}, u32[]{:S(2)}) collective-permute-start(bf16[512,128]{1,0:T(8,128)(2,1)} %apply.1.refs_0_), channel_id=1, source_target_pairs={{0,6},{1,7},{2,4},{3,5},{4,2},{5,3},{6,0},{7,1},{8,14},{9,15},{10,... | collective-permute-start | bytes 393224 | tf_op jit(solution)/shard_map/ppermute | solution.py:84
  95.7 6.0 %collective-permute-start.14 = (bf16[512,128]{1,0:T(8,128)(2,1)}, bf16[512,128]{1,0:T(8,128)(2,1)S(1)}, u32[]{:S(2)}, u32[]{:S(2)}) collective-permute-start(bf16[512,128]{1,0:T(8,128)(2,1)} %apply.1.refs_0_), channel_id=1, source_target_pairs={{0,4},{1,5},{2,6},{3,7},{4,0},{5,1},{6,2},{7,3},{8,12},{9,13},{10,... | collective-permute-start | bytes 393224 | tf_op jit(solution)/shard_map/ppermute | solution.py:84
  97.2 5.2 %collective-permute-start.13 = (bf16[512,128]{1,0:T(8,128)(2,1)}, bf16[512,128]{1,0:T(8,128)(2,1)S(1)}, u32[]{:S(2)}, u32[]{:S(2)}) collective-permute-start(bf16[512,128]{1,0:T(8,128)(2,1)} %apply.1.refs_0_), channel_id=1, source_target_pairs={{0,2},{1,3},{2,0},{3,1},{4,6},{5,7},{6,4},{7,5},{8,10},{9,11},{10,... | collective-permute-start | bytes 393224 | tf_op jit(solution)/shard_map/ppermute | solution.py:84
  97.8 4.6 %collective-permute-start.16 = (bf16[512,128]{1,0:T(8,128)(2,1)}, bf16[512,128]{1,0:T(8,128)(2,1)S(1)}, u32[]{:S(2)}, u32[]{:S(2)}) collective-permute-start(bf16[512,128]{1,0:T(8,128)(2,1)} %apply.1.refs_0_), channel_id=1, source_target_pairs={{0,1},{1,0},{2,3},{3,2},{4,5},{5,4},{6,7},{7,6},{8,9},{9,8},{10,11... | collective-permute-start | bytes 393224 | tf_op jit(solution)/shard_map/ppermute | solution.py:84
  100.4 3.3 %copy-start.8 = (bf16[512,128]{1,0:T(8,128)(2,1)}, bf16[512,128]{1,0:T(8,128)(2,1)S(1)}, u32[]{:S(2)}) copy-start(bf16[512,128]{1,0:T(8,128)(2,1)S(1)} %collective-permute-done.15.refs_3_) | copy-start | bytes 393220
  100.4 2.0 %collective-permute-start.19 = (bf16[512,128]{1,0:T(8,128)(2,1)S(1)}, bf16[512,128]{1,0:T(8,128)(2,1)S(1)}, u32[]{:S(2)}, u32[]{:S(2)}) collective-permute-start(bf16[512,128]{1,0:T(8,128)(2,1)S(1)} %collective-permute-done.15.refs_3_), channel_id=1, source_target_pairs={{0,1},{1,0},{2,3},{3,2},{4,5},{5,4},{6,7},{7,6},{8,9},{9,8},{10,11... | collective-permute-start | bytes 393224 | tf_op jit(solution)/shard_map/ppermute | solution.py:84
  101.7 2.0 %copy-start.9 = (bf16[512,128]{1,0:T(8,128)(2,1)}, bf16[512,128]{1,0:T(8,128)(2,1)S(1)}, u32[]{:S(2)}) copy-start(bf16[512,128]{1,0:T(8,128)(2,1)S(1)} %collective-permute-done.14.refs_2_) | copy-start | bytes 393220
  101.7 1.3 %collective-permute-start.18 = (bf16[512,128]{1,0:T(8,128)(2,1)S(1)}, bf16[512,128]{1,0:T(8,128)(2,1)S(1)}, u32[]{:S(2)}, u32[]{:S(2)}) collective-permute-start(bf16[512,128]{1,0:T(8,128)(2,1)S(1)} %collective-permute-done.14.refs_2_), channel_id=1, source_target_pairs={{0,1},{1,0},{2,3},{3,2},{4,5},{5,4},{6,7},{7,6},{8,9},{9,8},{10,11... | collective-permute-start | bytes 393224 | tf_op jit(solution)/shard_map/ppermute | solution.py:84
  102.4 1.4 %copy-start.10 = (bf16[512,128]{1,0:T(8,128)(2,1)}, bf16[512,128]{1,0:T(8,128)(2,1)S(1)}, u32[]{:S(2)}) copy-start(bf16[512,128]{1,0:T(8,128)(2,1)S(1)} %collective-permute-done.13.refs_1_) | copy-start | bytes 393220
  102.4 1.3 %collective-permute-start.17 = (bf16[512,128]{1,0:T(8,128)(2,1)S(1)}, bf16[512,128]{1,0:T(8,128)(2,1)S(1)}, u32[]{:S(2)}, u32[]{:S(2)}) collective-permute-start(bf16[512,128]{1,0:T(8,128)(2,1)S(1)} %collective-permute-done.13.refs_1_), channel_id=1, source_target_pairs={{0,1},{1,0},{2,3},{3,2},{4,5},{5,4},{6,7},{7,6},{8,9},{9,8},{10,11... | collective-permute-start | bytes 393224 | tf_op jit(solution)/shard_map/ppermute | solution.py:84
  102.4 1.4 %copy-start.11 = (bf16[512,128]{1,0:T(8,128)(2,1)}, bf16[512,128]{1,0:T(8,128)(2,1)S(1)}, u32[]{:S(2)}) copy-start(bf16[512,128]{1,0:T(8,128)(2,1)S(1)} %collective-permute-done.16.refs_4_) | copy-start | bytes 393220
  102.4 1.3 %copy-start.12 = (bf16[512,128]{1,0:T(8,128)(2,1)}, bf16[512,128]{1,0:T(8,128)(2,1)S(1)}, u32[]{:S(2)}) copy-start(bf16[512,128]{1,0:T(8,128)(2,1)S(1)} %collective-permute-done.19.refs_7_) | copy-start | bytes 393220
  (3 other events, 2.0 us)

commit v2 on v0

--- a/solution.py
+++ b/solution.py
@@ -1,12 +1,16 @@
+import functools
 import math
 
 import jax
 import jax.numpy as jnp
 from jax import lax
+from jax.experimental import pallas as pl
+from jax.experimental.pallas import tpu as pltpu
 from jax.sharding import PartitionSpec as P
 
 COLS_DONE = 8
-
+LANES = 128
+LOW = 256
 
 epsilon = 1e-06
 
@@ -23,7 +27,7 @@
     return jnp.take(table_rows, chosen_rows, axis=0)
 
 
-def on_device(design, row_signs, kept_rows):
+def plain_form(design, row_signs, kept_rows):
     block_count, local_rows, columns = design.shape
     keep_count = kept_rows.shape[1]
     groups = lax.axis_size("grp")
@@ -72,11 +76,337 @@
         vector = column - head_value * is_pivot
         return current - vector[:, None] * (2.0 * projected_row / length)[None, :]
 
-    result = lax.fori_loop(0, COLS_DONE, reflect, sketch)
-    return result
+    return lax.fori_loop(0, COLS_DONE, reflect, sketch)
+
+
+def swap(value, axis, mask):
+    pairs = [(place, place ^ mask) for place in range(lax.axis_size(axis))]
+    return lax.ppermute(value, axis, pairs)
+
+
+def odd_ones(bits):
+    bits = bits ^ (bits >> 2)
+    bits = bits ^ (bits >> 1)
+    return bits & 1
+
+
+def low_hadamard(shift):
+    row = lax.broadcasted_iota(jnp.int32, (LOW, LOW), 0)
+    col = lax.broadcasted_iota(jnp.int32, (LOW, LOW), 1)
+    signs = 1 - 2 * odd_ones((row & col) >> shift & 15)
+    same = ((row ^ col) & (255 - (15 << shift))) == 0
+    return jnp.where(same, signs, 0).astype(jnp.float32)
+
+
+def resident(kernel, name, outs, args, scratch=(), spaces=None, out_spaces=None, mebibytes=16):
+    here = pl.BlockSpec(memory_space=pltpu.VMEM)
+    return pl.pallas_call(
+        kernel,
+        out_shape=outs,
+        in_specs=spaces or [here] * len(args),
+        out_specs=out_spaces or (here,) * len(outs),
+        scratch_shapes=scratch,
+        compiler_params=pltpu.CompilerParams(vmem_limit_bytes=mebibytes << 20),
+        name=name,
+    )(*args)
+
+
+def front_kernel(kept_far, signs_far, data_ref, mixed_ref, table_ref, panel_ref, kept_ref, signs_ref, raw_ref, arrived):
+    keep = kept_ref.shape[1]
+    pieces = mixed_ref.shape[0] // LOW
+    small = [
+        pltpu.make_async_copy(kept_far, kept_ref, arrived.at[pieces]),
+        pltpu.make_async_copy(signs_far, signs_ref, arrived.at[pieces + 1]),
+    ]
+    copies = []
+    for piece in range(pieces):
+        rows = pl.ds(piece * LOW, LOW)
+        copies.append(pltpu.make_async_copy(data_ref.at[0, rows, :], raw_ref.at[rows, :], arrived.at[piece]))
+    for copy in small + copies:
+        copy.start()
+    for copy in small:
+        copy.wait()
+    first_piece = lax.axis_index("grp") * pieces
+    kept = jnp.broadcast_to(kept_ref[...], (8, keep))
+    line = lax.broadcasted_iota(jnp.int32, kept.shape, 0)
+    signs = 1 - 2 * odd_ones((kept >> 8) & (first_piece + line))
+    packed = jnp.where(line < pieces, signs, kept & 255).astype(jnp.float32)
+    step = 512
+    for start in range(0, keep, step):
+        tall = packed[:, start : start + step].T
+        lane = lax.broadcasted_iota(jnp.int32, (step, LOW), 1).astype(jnp.float32)
+        hit = tall[:, pieces : pieces + 1] == lane
+        for piece in range(pieces):
+            part = jnp.where(hit, tall[:, piece : piece + 1], 0.0).astype(jnp.bfloat16)
+            table_ref[start : start + step, piece * LOW : (piece + 1) * LOW] = part
+    inner_table = low_hadamard(0)
+    outer_table = low_hadamard(4).astype(jnp.bfloat16)
+    leads = []
+    for piece in range(pieces):
+        rows = slice(piece * LOW, (piece + 1) * LOW)
+        flips = (1 - 2 * signs_ref[:, rows]).astype(jnp.float32)
+        table = (inner_table * flips).astype(jnp.bfloat16)
+        copies[piece].wait()
+        first = jnp.dot(table, raw_ref[rows, :].astype(jnp.bfloat16), preferred_element_type=jnp.float32)
+        second = jnp.dot(outer_table, first.astype(jnp.bfloat16), preferred_element_type=jnp.float32)
+        second = second.astype(jnp.bfloat16)
+        mixed_ref[rows, :] = second
+        leads.append(second[:, :LANES].astype(jnp.float32).T[:16].astype(jnp.bfloat16))
+    lead = jnp.concatenate(leads, axis=1)
+    for start in range(0, keep, step):
+        rows = slice(start, start + step)
+        part = lax.dot_general(
+            lead, table_ref[rows, :], (((1,), (1,)), ((), ())), preferred_element_type=jnp.float32
+        )
+        panel_ref[:, rows] = part[:COLS_DONE]
+
+
+def front(kept, signs, design):
+    _, rows, columns = design.shape
+    keep = kept.shape[1]
+    outs = (
+        pltpu.VMEM((rows, columns), jnp.bfloat16),
+        pltpu.VMEM((keep, rows), jnp.bfloat16),
+        pltpu.VMEM((COLS_DONE, keep), jnp.float32),
+    )
+    scratch = [
+        pltpu.VMEM(kept.shape, jnp.int32),
+        pltpu.VMEM(signs.shape, jnp.int32),
+        pltpu.VMEM((rows, columns), jnp.float32),
+        pltpu.SemaphoreType.DMA((rows // LOW + 2,)),
+    ]
+    spaces = [pl.BlockSpec(memory_space=pltpu.HBM)] * 3
+    return resident(front_kernel, "front", outs, (kept, signs, design), scratch, spaces, mebibytes=56)
+
+
+def addend_kernel(masks, width, has_arrived, has_panel, table_ref, mixed_ref, *refs):
+    refs = list(refs)
+    arrived = [refs.pop(0) for _ in masks] if has_arrived else []
+    panels = [refs.pop(0) for _ in range(2)] if has_panel else []
+    member = lax.axis_index("inner")
+    if has_panel:
+        refs.pop()[...] = panels[0][...] + panels[1][...]
+    parts = []
+    for mask in masks:
+        parts.append(mixed_ref[:, pl.ds(pl.multiple_of((member ^ mask) * width, width), width)])
+    part = jnp.dot(table_ref[...], jnp.concatenate(parts, axis=1), preferred_element_type=jnp.float32)
+    for index, out_ref in enumerate(refs):
+        value = part[:, index * width : (index + 1) * width]
+        if arrived:
+            value = value + arrived[index][...].astype(jnp.float32)
+        out_ref[...] = value.astype(out_ref.dtype)
+
+
+def addend(table, mixed, masks, width, dtypes, arrived=(), panels=()):
+    keep = table.shape[0]
+    outs = tuple(pltpu.VMEM((keep, width), dtype) for dtype in dtypes)
+    outs += tuple(pltpu.VMEM(panel.shape, panel.dtype) for panel in panels[:1])
+    kernel = functools.partial(addend_kernel, masks, width, bool(arrived), bool(panels))
+    return resident(kernel, "addend", outs, (table, mixed, *arrived, *panels))
+
+
+def factor_kernel(scale, panel_ref, other_ref, vectors_ref, weights_ref):
+    current = (panel_ref[...] + other_ref[...]) * scale
+    count, keep = current.shape
+    lane = lax.broadcasted_iota(jnp.int32, (1, keep), 1)
+    line = lax.broadcasted_iota(jnp.int32, (count, 1), 0)
+    short = lax.broadcasted_iota(jnp.int32, (1, LANES), 1)
+    vectors = jnp.zeros((count, keep), jnp.float32)
+    weights = jnp.zeros((count, LANES), jnp.float32)
+    for j in range(count):
+        column = jnp.where(lane >= j, current[j : j + 1, :], 0.0)
+        is_pivot = lane == j
+        crossed = jnp.sum(current * column, axis=1, keepdims=True)
+        pivot_row = jnp.sum(jnp.where(is_pivot, current, 0.0), axis=1, keepdims=True)
+        norm_sq = crossed[j : j + 1, :]
+        pivot = pivot_row[j : j + 1, :]
+        head = jnp.where(pivot >= 0, -1.0, 1.0) * jnp.sqrt(norm_sq)
+        length = 2.0 * (norm_sq - head * pivot) + epsilon
+        vector = column - jnp.where(is_pivot, head, 0.0)
+        projected = crossed - head * pivot_row
+        current = current - (2.0 * projected / length) * vector
+        shared = jnp.sum(vectors * vector, axis=1, keepdims=True)
+        unit = jnp.where(short == j, 1.0, 0.0)
+        row = (2.0 / length) * (unit - jnp.sum(shared * weights, axis=0, keepdims=True))
+        vectors = jnp.where(line == j, vector, vectors)
+        weights = jnp.where(line == j, row, weights)
+    vectors_ref[...] = vectors
+    weights_ref[...] = weights
+
+
+def factor(panel, other, scale):
+    count, keep = panel.shape
+    outs = (pltpu.VMEM((count, keep), jnp.float32), pltpu.VMEM((count, LANES), jnp.float32))
+    return resident(functools.partial(factor_kernel, scale), "factor", outs, (panel, other))
+
+
+def split_two(value):
+    high = value.astype(jnp.bfloat16)
+    low = (value - high.astype(jnp.float32)).astype(jnp.bfloat16)
+    return jnp.concatenate([high, low], axis=0)
+
+
+def spread_kernel(scale, arrived_count, vectors_ref, base_ref, *refs):
+    arrived, outs = refs[:arrived_count], refs[arrived_count:]
+    *send_refs, own_ref, product_ref = outs
+    rows = own_ref.shape[0]
+    count = vectors_ref.shape[0]
+    group = lax.axis_index("grp")
+
+    def total(window):
+        value = base_ref[window, :]
+        for ref in arrived:
+            value = value + ref[window, :].astype(jnp.float32)
+        return value * scale
+
+    both = jnp.zeros((2 * count, own_ref.shape[1]), jnp.float32)
+    for index in range(len(send_refs) + 1):
+        start = pl.multiple_of((group ^ index) * rows, rows)
+        value = total(pl.ds(start, rows))
+        short = value.astype(jnp.bfloat16)
+        if index:
+            send_refs[index - 1][:rows, :] = short
+        else:
+            own_ref[...] = value
+        pair = split_two(vectors_ref[:, pl.ds(start, rows)])
+        both = both + jnp.dot(pair, short, preferred_element_type=jnp.float32)
+    product = both[:count] + both[count:]
+    product_ref[...] = product
+    pair = split_two(product)
+    for send_ref in send_refs:
+        send_ref[rows:, :] = pair
+
+
+def spread(vectors, base, arrived, groups, scale):
+    keep, width = base.shape
+    count = vectors.shape[0]
+    rows = keep // groups
+    outs = [pltpu.VMEM((rows + 2 * count, width), jnp.bfloat16)] * (groups - 1)
+    outs += [pltpu.VMEM((rows, width), jnp.float32), pltpu.VMEM((count, width), jnp.float32)]
+    kernel = functools.partial(spread_kernel, scale, len(arrived))
+    return resident(kernel, "spread", tuple(outs), (vectors, base, *arrived))
+
+
+def apply_kernel(vectors_ref, weights_ref, own_ref, product_ref, *refs):
+    *arrived, out_ref = refs
+    rows = own_ref.shape[0]
+    count = vectors_ref.shape[0]
+    value = own_ref[...]
+    product = product_ref[...]
+    for ref in arrived:
+        value = value + ref[:rows, :].astype(jnp.float32)
+        pair = ref[rows:, :].astype(jnp.float32)
+        product = product + (pair[:count] + pair[count:])
+    highest = lax.Precision.HIGHEST
+    multipliers = jnp.dot(
+        weights_ref[:, :count], product, precision=highest, preferred_element_type=jnp.float32
+    )
+    window = pl.ds(pl.multiple_of(lax.axis_index("grp") * rows, rows), rows)
+    vectors = vectors_ref[:, window]
+    update = lax.dot_general(
+        vectors, multipliers, (((0,), (0,)), ((), ())), precision=highest, preferred_element_type=jnp.float32
+    )
+    out_ref[...] = (value - update).astype(jnp.bfloat16)
+
+
+def apply(vectors, weights, own, product, arrived):
+    outs = (pltpu.VMEM(own.shape, jnp.bfloat16),)
+    return resident(apply_kernel, "apply", outs, (vectors, weights, own, product, *arrived))[0]
+
+
+def lay_kernel(masks, *refs):
+    parts, (out_ref, wide_ref, left) = refs[: len(masks)], refs[len(masks) :]
+    width = parts[0].shape[1]
+    copies = []
+    for index, mask in enumerate(masks):
+        start = pl.multiple_of((lax.axis_index("inner") ^ mask) * width, width)
+        wide_ref[index] = parts[index][...].astype(jnp.float32)
+        copies.append(
+            pltpu.make_async_copy(wide_ref.at[index], out_ref.at[:, pl.ds(start, width)], left.at[index])
+        )
+        copies[-1].start()
+    for copy in copies:
+        copy.wait()
+
+
+def lay(parts, masks):
+    rows, width = parts[0].shape
+    outs = (jax.ShapeDtypeStruct((rows, width * len(parts)), jnp.float32),)
+    scratch = [pltpu.VMEM((len(parts), rows, width), jnp.float32), pltpu.SemaphoreType.DMA((len(parts),))]
+    away = (pl.BlockSpec(memory_space=pl.ANY),)
+    return resident(functools.partial(lay_kernel, masks), "lay", outs, parts, scratch, None, away)[0]
+
+
+def wide_form(design, row_signs, kept_rows):
+    columns = design.shape[2]
+    keep = kept_rows.shape[1]
+    groups, members = lax.axis_size("grp"), lax.axis_size("inner")
+    width = columns // members
+    scale = 1.0 / (64.0 * math.sqrt(keep))
+    short, full = jnp.bfloat16, jnp.float32
+    mixed, table, panel = front(kept_rows, row_signs, design)
+
+    steps = [("inner", 1 << bit) for bit in range(members.bit_length() - 1)]
+    steps += [("grp", 1 << bit) for bit in range(groups.bit_length() - 1)]
+    far = list(range(2, members, 2))
+    order = far + [0]
+    pairs = [order[start : start + 2] for start in range(0, len(order), 2)]
+    work = [([mask ^ 1 for mask in pair], [short] * 2, None) for pair in pairs]
+    work += [(pair, [short if mask else full for mask in pair], index) for index, pair in enumerate(pairs)]
+    arrived, sums = [], {}
+    waiting = swap(panel, *steps.pop(0))
+    for turn, (masks, dtypes, index) in enumerate(work):
+        panels = (panel, waiting) if turn and len(steps) > 1 else ()
+        got = arrived[index] if index is not None else ()
+        values = list(addend(table, mixed, masks, width, dtypes, got, panels))
+        if panels:
+            panel = values.pop()
+            waiting = swap(panel, *steps.pop(0))
+        if index is None:
+            arrived.append([swap(value, "inner", 1) for value in values])
+        else:
+            sums.update(zip(masks, values))
+    moved = [swap(sums[mask], "inner", mask) for mask in far]
+    while steps:
+        panel = panel + waiting
+        waiting = swap(panel, *steps.pop(0))
+    vectors, weights = factor(panel, waiting, scale)
+
+    *sends, own, product = spread(vectors, sums[0], moved, groups, scale)
+    got = [swap(value, "grp", index + 1) for index, value in enumerate(sends)]
+    done = apply(vectors, weights, own, product, got)
+    parts = [done] + [swap(done, "inner", mask) for mask in far]
+    masks = [0] + far
+    parts += [swap(part, "inner", 1) for part in parts]
+    masks += [mask ^ 1 for mask in masks]
+    return lay(parts, masks)
+
+
+def power_of_two(size):
+    return size & (size - 1) == 0
 
 
 def solution(mesh):
+    groups, members = mesh.shape["grp"], mesh.shape["inner"]
+
+    def on_device(design, row_signs, kept_rows):
+        block_count, local_rows, columns = design.shape
+        keep = kept_rows.shape[1]
+        fits = (
+            block_count == 1
+            and power_of_two(groups)
+            and power_of_two(members)
+            and members >= 4
+            and groups >= 2
+            and columns % (members * LANES) == 0
+            and local_rows % LOW == 0
+            and local_rows // LOW < 8
+            and keep % (groups * LANES) == 0
+            and keep % 512 == 0
+        )
+        form = wide_form if fits else plain_form
+        return form(design, row_signs, kept_rows)
+
     return jax.shard_map(
         on_device,
         mesh=mesh,

time: 398 us -> 67.9 us (0.17)
  waiting for transfers between devices: 156 us -> 29.2 us
  blocking collectives: 82.7 us -> 0 us
  local copies, waits for them, and re-layouts: 56 us -> 0 us
  matrix products: 28 us -> 0 us
  other arithmetic: 27.4 us -> 0.01 us
  loops' own time: 22.4 us -> 0 us
  Pallas kernels: 0 us -> 14 us
  between operations: 13.5 us -> 0.08 us
  starting transfers between devices: 11 us -> 24.3 us
    all_to_all x2 -> x0, waiting for transfers between devices: 95.2 us -> none  [the longest x1 48.1 us: on_device(): lax.all_to_all(second_pass, 'grp', split_axis=2, concat_axis=1, tiled=True)]
    psum x8 -> x0, blocking collectives: 82.7 us -> none  [reflect(): lax.psum((jnp.sum(column * column), jnp.dot(column, current, precision=hi...]
    psum x1 -> x0, waiting for transfers between devices: 61 us -> none  [on_device(): summed = lax.psum(partial_value, 'inner')]
    ppermute x0 -> x22, waiting for transfers between devices: none -> 29.2 us  [swap(): return lax.ppermute(value, axis, pairs)]
    dot_general x19 -> x0, matrix products: 28 us -> none  [the longest x8 14.5 us: reflect(): jnp.dot(column, current, precision=highest)]
    ppermute x0 -> x22, starting transfers between devices: none -> 24.3 us  [swap(): return lax.ppermute(value, axis, pairs)]
    another operation x1 -> x0, loops' own time: 22.4 us -> none  [on_device(): result = lax.fori_loop(0, COLS_DONE, reflect, sketch)]
    gather x2 -> x0, local copies, waits for them, and re-layouts: 21.4 us -> none  [pick_rows(): return jnp.take(table_rows, chosen_rows, axis=0)]
  transfers between devices with their start and end apart: 3 -> 22, of which waited for: 3 -> 12; matrix products, arithmetic and copies ran while one was open for 0% -> 0% of each run, Pallas kernels for 0% -> 9%
where the time goes in v2:
time: 67.9 us; the launch traced here: 67.7 us
  waiting for transfers between devices  29.2 us (43%)
  starting transfers between devices  24.3 us (36%)
  Pallas kernels  14 us (21%)
    ppermute x22, waiting for transfers between devices, swap(): return lax.ppermute(value, axis, pairs)  29.2 us
    ppermute x22, starting transfers between devices, swap(): return lax.ppermute(value, axis, pairs)  24.3 us
    pallas_call x9, Pallas kernels, resident(): pl.pallas_call(kernel, out_shape=outs, in_specs=spaces or [here] * len(ar...  14 us
  transfers between devices with their start and end apart: 22, of which 12 were waited for; matrix products, arithmetic and copies ran while one was open for 0% of the time, Pallas kernels for 9%

profile of v2, /device:TPU:0, one launch (start us, length us, event | category | flops | bytes accessed | tf_op | source)
XLA Modules:
  0.0 67.7 jit_solution(14654932047350292516)
XLA Ops:
  0.0 5.5 %front.1 = (bf16[1024,1024]{1,0:T(8,128)(2,1)S(1)}, bf16[2048,1024]{1,0:T(8,128)(2,1)S(1)}, f32[8,2048]{1,0:T(8,128)S(1)}) custom-call(s32[1,2048]{1,0:T(1,128)} %kept_far.1, s32[1,1024]{1,0:T(1,128)} %signs_far.1, f32[1,1024,1024]{2,1,0:T(8,128)} %data_ref.1), custom_call_target="tpu_custom_call" | custom-call | tf_op jit(solution)/shard_map/front/pallas_call | solution.py:103
  5.5 0.6 collective-permute-start
  6.1 1.3 %addend.5 = (bf16[2048,128]{1,0:T(8,128)(2,1)S(1)}, bf16[2048,128]{1,0:T(8,128)(2,1)S(1)}) custom-call(bf16[2048,1024]{1,0:T(8,128)(2,1)S(1)} %get-tuple-element.26.table_ref, bf16[1024,1024]{1,0:T(8,128)(2,1)S(1)} %get-tuple-element.27.mixed_ref), custom_call_target="tpu_custom_call" | custom-call | tf_op jit(solution)/shard_map/addend/pallas_call | solution.py:103
  8.0 1.3 %addend.4 = (bf16[2048,128]{1,0:T(8,128)(2,1)S(1)}, bf16[2048,128]{1,0:T(8,128)(2,1)S(1)}, f32[8,2048]{1,0:T(8,128)S(1)}) custom-call(bf16[2048,1024]{1,0:T(8,128)(2,1)S(1)} %get-tuple-element.26.table_ref, bf16[1024,1024]{1,0:T(8,128)(2,1)S(1)} %get-tuple-element.27.mixed_ref, f32[8,2048]{1,0:T(8,128)S(1)} %get-tuple-element.28.refs_0_, ...), custom_call_target="tpu_custom_call" | custom-call | tf_op jit(solution)/shard_map/addend/pallas_call | solution.py:103
  9.8 2.5 %collective-permute-start.5 = (f32[8,2048]{1,0:T(8,128)S(1)}, f32[8,2048]{1,0:T(8,128)S(1)}, u32[]{:S(2)}, u32[]{:S(2)}) collective-permute-start(f32[8,2048]{1,0:T(8,128)S(1)} %get-tuple-element.33.refs_2_), channel_id=1, source_target_pairs={{0,2},{1,3},{2,0},{3,1},{4,6},{5,7},{6,4},{7,5},{8,10},{9,11},{10,... | collective-permute-start | bytes 196616 | tf_op jit(solution)/shard_map/ppermute | solution.py:84
  12.4 2.7 %collective-permute-done.5.refs_3_ = f32[8,2048]{1,0:T(8,128)S(1)} collective-permute-done((f32[8,2048]{1,0:T(8,128)S(1)}, f32[8,2048]{1,0:T(8,128)S(1)}, u32[]{:S(2)}, u32[]{:S(2)}) %collective-permute-start.5) | collective-permute-done | bytes 65568 | tf_op jit(solution)/shard_map/ppermute | solution.py:84
  15.1 1.3 %addend.6 = (bf16[2048,128]{1,0:T(8,128)(2,1)S(1)}, bf16[2048,128]{1,0:T(8,128)(2,1)S(1)}, f32[8,2048]{1,0:T(8,128)S(1)}) custom-call(bf16[2048,1024]{1,0:T(8,128)(2,1)S(1)} %get-tuple-element.26.table_ref, bf16[1024,1024]{1,0:T(8,128)(2,1)S(1)} %get-tuple-element.27.mixed_ref, bf16[2048,128]{1,0:T(8,128)(2,1)S(1)} %collective-permute-done.3.refs_0_, ...), custom_call_target="tpu_custom_call" | custom-call | tf_op jit(solution)/shard_map/addend/pallas_call | solution.py:103
  16.4 1.8 %collective-permute-start.6 = (f32[8,2048]{1,0:T(8,128)S(1)}, f32[8,2048]{1,0:T(8,128)S(1)}, u32[]{:S(2)}, u32[]{:S(2)}) collective-permute-start(f32[8,2048]{1,0:T(8,128)S(1)} %get-tuple-element.34.refs_2_), channel_id=1, source_target_pairs={{0,4},{1,5},{2,6},{3,7},{4,0},{5,1},{6,2},{7,3},{8,12},{9,13},{10,... | collective-permute-start | bytes 196616 | tf_op jit(solution)/shard_map/ppermute | solution.py:84
  18.2 1.5 %collective-permute-start.9 = (bf16[2048,128]{1,0:T(8,128)(2,1)S(1)}, bf16[2048,128]{1,0:T(8,128)(2,1)S(1)}, u32[]{:S(2)}, u32[]{:S(2)}) collective-permute-start(bf16[2048,128]{1,0:T(8,128)(2,1)S(1)} %get-tuple-element.39), channel_id=1, source_target_pairs={{0,2},{1,3},{2,0},{3,1},{4,6},{5,7},{6,4},{7,5},{8,10},{9,11},{10,... | collective-permute-start | bytes 1572872 | tf_op jit(solution)/shard_map/ppermute | solution.py:84
  20.2 0.5 collective-permute-done.6.refs_3_
  20.7 1.3 %addend.7 = (bf16[2048,128]{1,0:T(8,128)(2,1)S(1)}, f32[2048,128]{1,0:T(8,128)S(1)}, f32[8,2048]{1,0:T(8,128)S(1)}) custom-call(bf16[2048,1024]{1,0:T(8,128)(2,1)S(1)} %get-tuple-element.26.table_ref, bf16[1024,1024]{1,0:T(8,128)(2,1)S(1)} %get-tuple-element.27.mixed_ref, bf16[2048,128]{1,0:T(8,128)(2,1)S(1)} %collective-permute-done.1.refs_0_, ...), custom_call_target="tpu_custom_call" | custom-call | tf_op jit(solution)/shard_map/addend/pallas_call | solution.py:103
  22.1 3.5 %collective-permute-start.11 = (bf16[2048,128]{1,0:T(8,128)(2,1)S(1)}, bf16[2048,128]{1,0:T(8,128)(2,1)S(1)}, u32[]{:S(2)}, u32[]{:S(2)}) collective-permute-start(bf16[2048,128]{1,0:T(8,128)(2,1)S(1)} %get-tuple-element.41), channel_id=1, source_target_pairs={{0,6},{1,7},{2,4},{3,5},{4,2},{5,3},{6,0},{7,1},{8,14},{9,15},{10,... | collective-permute-start | bytes 1572872 | tf_op jit(solution)/shard_map/ppermute | solution.py:84
  25.5 1.6 %collective-permute-start.7 = (f32[8,2048]{1,0:T(8,128)S(1)}, f32[8,2048]{1,0:T(8,128)S(1)}, u32[]{:S(2)}, u32[]{:S(2)}) collective-permute-start(f32[8,2048]{1,0:T(8,128)S(1)} %get-tuple-element.35), channel_id=1, source_target_pairs={{0,8},{8,0},{16,24},{24,16},{1,9},{9,1},{17,25},{25,17},{2,10},{10... | collective-permute-start | bytes 196616 | tf_op jit(solution)/shard_map/ppermute | solution.py:84
  27.1 2.7 %collective-permute-done.7 = f32[8,2048]{1,0:T(8,128)S(1)} collective-permute-done((f32[8,2048]{1,0:T(8,128)S(1)}, f32[8,2048]{1,0:T(8,128)S(1)}, u32[]{:S(2)}, u32[]{:S(2)}) %collective-permute-start.7) | collective-permute-done | bytes 65568 | tf_op jit(solution)/shard_map/ppermute | solution.py:84
  29.8 3.2 %collective-permute-start.8 = (f32[8,2048]{1,0:T(8,128)S(1)}, f32[8,2048]{1,0:T(8,128)S(1)}, u32[]{:S(2)}, u32[]{:S(2)}) collective-permute-start(f32[8,2048]{1,0:T(8,128)S(1)} %add.3.panel_ref), channel_id=1, source_target_pairs={{0,16},{8,24},{16,0},{24,8},{1,17},{9,25},{17,1},{25,9},{2,18},{10... | collective-permute-start | bytes 196616 | tf_op jit(solution)/shard_map/ppermute | solution.py:84
  33.0 2.2 %collective-permute-done.8.other_ref = f32[8,2048]{1,0:T(8,128)S(1)} collective-permute-done((f32[8,2048]{1,0:T(8,128)S(1)}, f32[8,2048]{1,0:T(8,128)S(1)}, u32[]{:S(2)}, u32[]{:S(2)}) %collective-permute-start.8) | collective-permute-done | bytes 65568 | tf_op jit(solution)/shard_map/ppermute | solution.py:84
  35.2 1.0 %factor.1 = (f32[8,2048]{1,0:T(8,128)S(1)}, f32[8,128]{1,0:T(8,128)S(1)}) custom-call(f32[8,2048]{1,0:T(8,128)S(1)} %add.3.panel_ref, f32[8,2048]{1,0:T(8,128)S(1)} %collective-permute-done.8.other_ref), custom_call_target="tpu_custom_call" | custom-call | tf_op jit(solution)/shard_map/factor/pallas_call | solution.py:103
  36.3 7.5 %collective-permute-done.10.refs_1_ = bf16[2048,128]{1,0:T(8,128)(2,1)S(1)} collective-permute-done((bf16[2048,128]{1,0:T(8,128)(2,1)S(1)}, bf16[2048,128]{1,0:T(8,128)(2,1)S(1)}, u32[]{:S(2)}, u32[]{:S(2)}) %collective-permute-start.10) | collective-permute-done | bytes 524320 | tf_op jit(solution)/shard_map/ppermute | solution.py:84
  44.2 1.6 %collective-permute-start.12 = (bf16[528,128]{1,0:T(8,128)(2,1)S(1)}, bf16[528,128]{1,0:T(8,128)(2,1)S(1)}, u32[]{:S(2)}, u32[]{:S(2)}) collective-permute-start(bf16[528,128]{1,0:T(8,128)(2,1)S(1)} %get-tuple-element.44), channel_id=1, source_target_pairs={{0,8},{8,0},{16,24},{24,16},{1,9},{9,1},{17,25},{25,17},{2,10},{10... | collective-permute-start | bytes 405512 | tf_op jit(solution)/shard_map/ppermute | solution.py:84
  45.9 2.6 %collective-permute-start.13 = (bf16[528,128]{1,0:T(8,128)(2,1)S(1)}, bf16[528,128]{1,0:T(8,128)(2,1)S(1)}, u32[]{:S(2)}, u32[]{:S(2)}) collective-permute-start(bf16[528,128]{1,0:T(8,128)(2,1)S(1)} %get-tuple-element.45), channel_id=1, source_target_pairs={{0,16},{8,24},{16,0},{24,8},{1,17},{9,25},{17,1},{25,9},{2,18},{10... | collective-permute-start | bytes 405512 | tf_op jit(solution)/shard_map/ppermute | solution.py:84
  48.7 1.2 %collective-permute-done.12.refs_0_ = bf16[528,128]{1,0:T(8,128)(2,1)S(1)} collective-permute-done((bf16[528,128]{1,0:T(8,128)(2,1)S(1)}, bf16[528,128]{1,0:T(8,128)(2,1)S(1)}, u32[]{:S(2)}, u32[]{:S(2)}) %collective-permute-start.12) | collective-permute-done | bytes 135200 | tf_op jit(solution)/shard_map/ppermute | solution.py:84
  49.8 6.6 %collective-permute-done.13.refs_1_ = bf16[528,128]{1,0:T(8,128)(2,1)S(1)} collective-permute-done((bf16[528,128]{1,0:T(8,128)(2,1)S(1)}, bf16[528,128]{1,0:T(8,128)(2,1)S(1)}, u32[]{:S(2)}, u32[]{:S(2)}) %collective-permute-start.13) | collective-permute-done | bytes 135200 | tf_op jit(solution)/shard_map/ppermute | solution.py:84
  56.4 0.5 apply.1.refs_0_
  56.9 2.5 %collective-permute-start.17 = (bf16[512,128]{1,0:T(8,128)(2,1)S(1)}, bf16[512,128]{1,0:T(8,128)(2,1)S(1)}, u32[]{:S(2)}, u32[]{:S(2)}) collective-permute-start(bf16[512,128]{1,0:T(8,128)(2,1)S(1)} %apply.1.refs_0_), channel_id=1, source_target_pairs={{0,6},{1,7},{2,4},{3,5},{4,2},{5,3},{6,0},{7,1},{8,14},{9,15},{10,... | collective-permute-start | bytes 393224 | tf_op jit(solution)/shard_map/ppermute | solution.py:84
  59.4 0.5 collective-permute-start.16
  59.9 0.5 collective-permute-start.15
  60.5 2.4 %collective-permute-done.17.refs_3_ = bf16[512,128]{1,0:T(8,128)(2,1)S(1)} collective-permute-done((bf16[512,128]{1,0:T(8,128)(2,1)S(1)}, bf16[512,128]{1,0:T(8,128)(2,1)S(1)}, u32[]{:S(2)}, u32[]{:S(2)}) %collective-permute-start.17) | collective-permute-done | bytes 131104 | tf_op jit(solution)/shard_map/ppermute | solution.py:84
  62.9 1.5 %collective-permute-done.16.refs_2_ = bf16[512,128]{1,0:T(8,128)(2,1)S(1)} collective-permute-done((bf16[512,128]{1,0:T(8,128)(2,1)S(1)}, bf16[512,128]{1,0:T(8,128)(2,1)S(1)}, u32[]{:S(2)}, u32[]{:S(2)}) %collective-permute-start.16) | collective-permute-done | bytes 131104 | tf_op jit(solution)/shard_map/ppermute | solution.py:84
  64.4 0.5 collective-permute-done.15.refs_1_
  64.9 0.8 %collective-permute-done.20.refs_6_ = bf16[512,128]{1,0:T(8,128)(2,1)S(1)} collective-permute-done((bf16[512,128]{1,0:T(8,128)(2,1)S(1)}, bf16[512,128]{1,0:T(8,128)(2,1)S(1)}, u32[]{:S(2)}, u32[]{:S(2)}) %collective-permute-start.20) | collective-permute-done | bytes 131104 | tf_op jit(solution)/shard_map/ppermute | solution.py:84
  65.7 0.5 collective-permute-done.19.refs_5_
  66.3 1.4 %lay.1 = f32[512,1024]{1,0:T(8,128)} custom-call(bf16[512,128]{1,0:T(8,128)(2,1)S(1)} %apply.1.refs_0_, bf16[512,128]{1,0:T(8,128)(2,1)S(1)} %collective-permute-done.15.refs_1_, bf16[512,128]{1,0:T(8,128)(2,1)S(1)} %collective-permute-done.16.refs_2_, bf16[512,128]{1,0:T(8,128)(2,1)S(1)} %collective-permute-done.17.refs_3_, ...), custom_call_target="tpu_custom_call" | custom-call | tf_op jit(solution)/shard_map/lay/pallas_call | solution.py:103
  (22 shorter events, 2.3 us)
Async XLA Ops:
  5.5 2.5 %collective-permute-start = (f32[8,2048]{1,0:T(8,128)S(1)}, f32[8,2048]{1,0:T(8,128)S(1)}, u32[]{:S(2)}, u32[]{:S(2)}) collective-permute-start(f32[8,2048]{1,0:T(8,128)S(1)} %get-tuple-element.28.refs_0_), channel_id=1, source_target_pairs={{0,1},{1,0},{2,3},{3,2},{4,5},{5,4},{6,7},{7,6},{8,9},{9,8},{10,11... | collective-permute-start | bytes 196616 | tf_op jit(solution)/shard_map/ppermute | solution.py:84
  7.4 7.7 %collective-permute-start.3 = (bf16[2048,128]{1,0:T(8,128)(2,1)S(1)}, bf16[2048,128]{1,0:T(8,128)(2,1)S(1)}, u32[]{:S(2)}, u32[]{:S(2)}) collective-permute-start(bf16[2048,128]{1,0:T(8,128)(2,1)S(1)} %get-tuple-element.31), channel_id=1, source_target_pairs={{0,1},{1,0},{2,3},{3,2},{4,5},{5,4},{6,7},{7,6},{8,9},{9,8},{10,11... | collective-permute-start | bytes 1572872 | tf_op jit(solution)/shard_map/ppermute | solution.py:84
  7.5 7.6 %collective-permute-start.4 = (bf16[2048,128]{1,0:T(8,128)(2,1)S(1)}, bf16[2048,128]{1,0:T(8,128)(2,1)S(1)}, u32[]{:S(2)}, u32[]{:S(2)}) collective-permute-start(bf16[2048,128]{1,0:T(8,128)(2,1)S(1)} %get-tuple-element.32), channel_id=1, source_target_pairs={{0,1},{1,0},{2,3},{3,2},{4,5},{5,4},{6,7},{7,6},{8,9},{9,8},{10,11... | collective-permute-start | bytes 1572872 | tf_op jit(solution)/shard_map/ppermute | solution.py:84
  9.3 11.0 %collective-permute-start.1 = (bf16[2048,128]{1,0:T(8,128)(2,1)S(1)}, bf16[2048,128]{1,0:T(8,128)(2,1)S(1)}, u32[]{:S(2)}, u32[]{:S(2)}) collective-permute-start(bf16[2048,128]{1,0:T(8,128)(2,1)S(1)} %get-tuple-element.29), channel_id=1, source_target_pairs={{0,1},{1,0},{2,3},{3,2},{4,5},{5,4},{6,7},{7,6},{8,9},{9,8},{10,11... | collective-permute-start | bytes 1572872 | tf_op jit(solution)/shard_map/ppermute | solution.py:84
  9.4 10.8 %collective-permute-start.2 = (bf16[2048,128]{1,0:T(8,128)(2,1)S(1)}, bf16[2048,128]{1,0:T(8,128)(2,1)S(1)}, u32[]{:S(2)}, u32[]{:S(2)}) collective-permute-start(bf16[2048,128]{1,0:T(8,128)(2,1)S(1)} %get-tuple-element.30), channel_id=1, source_target_pairs={{0,1},{1,0},{2,3},{3,2},{4,5},{5,4},{6,7},{7,6},{8,9},{9,8},{10,11... | collective-permute-start | bytes 1572872 | tf_op jit(solution)/shard_map/ppermute | solution.py:84
  9.8 5.2 %collective-permute-start.5 = (f32[8,2048]{1,0:T(8,128)S(1)}, f32[8,2048]{1,0:T(8,128)S(1)}, u32[]{:S(2)}, u32[]{:S(2)}) collective-permute-start(f32[8,2048]{1,0:T(8,128)S(1)} %get-tuple-element.33.refs_2_), channel_id=1, source_target_pairs={{0,2},{1,3},{2,0},{3,1},{4,6},{5,7},{6,4},{7,5},{8,10},{9,11},{10,... | collective-permute-start | bytes 196616 | tf_op jit(solution)/shard_map/ppermute | solution.py:84
  16.4 4.3 %collective-permute-start.6 = (f32[8,2048]{1,0:T(8,128)S(1)}, f32[8,2048]{1,0:T(8,128)S(1)}, u32[]{:S(2)}, u32[]{:S(2)}) collective-permute-start(f32[8,2048]{1,0:T(8,128)S(1)} %get-tuple-element.34.refs_2_), channel_id=1, source_target_pairs={{0,4},{1,5},{2,6},{3,7},{4,0},{5,1},{6,2},{7,3},{8,12},{9,13},{10,... | collective-permute-start | bytes 196616 | tf_op jit(solution)/shard_map/ppermute | solution.py:84
  18.2 18.0 %collective-permute-start.9 = (bf16[2048,128]{1,0:T(8,128)(2,1)S(1)}, bf16[2048,128]{1,0:T(8,128)(2,1)S(1)}, u32[]{:S(2)}, u32[]{:S(2)}) collective-permute-start(bf16[2048,128]{1,0:T(8,128)(2,1)S(1)} %get-tuple-element.39), channel_id=1, source_target_pairs={{0,2},{1,3},{2,0},{3,1},{4,6},{5,7},{6,4},{7,5},{8,10},{9,11},{10,... | collective-permute-start | bytes 1572872 | tf_op jit(solution)/shard_map/ppermute | solution.py:84
  19.7 24.1 %collective-permute-start.10 = (bf16[2048,128]{1,0:T(8,128)(2,1)S(1)}, bf16[2048,128]{1,0:T(8,128)(2,1)S(1)}, u32[]{:S(2)}, u32[]{:S(2)}) collective-permute-start(bf16[2048,128]{1,0:T(8,128)(2,1)S(1)} %get-tuple-element.40), channel_id=1, source_target_pairs={{0,4},{1,5},{2,6},{3,7},{4,0},{5,1},{6,2},{7,3},{8,12},{9,13},{10,... | collective-permute-start | bytes 1572872 | tf_op jit(solution)/shard_map/ppermute | solution.py:84
  22.1 21.8 %collective-permute-start.11 = (bf16[2048,128]{1,0:T(8,128)(2,1)S(1)}, bf16[2048,128]{1,0:T(8,128)(2,1)S(1)}, u32[]{:S(2)}, u32[]{:S(2)}) collective-permute-start(bf16[2048,128]{1,0:T(8,128)(2,1)S(1)} %get-tuple-element.41), channel_id=1, source_target_pairs={{0,6},{1,7},{2,4},{3,5},{4,2},{5,3},{6,0},{7,1},{8,14},{9,15},{10,... | collective-permute-start | bytes 1572872 | tf_op jit(solution)/shard_map/ppermute | solution.py:84
  25.5 4.3 %collective-permute-start.7 = (f32[8,2048]{1,0:T(8,128)S(1)}, f32[8,2048]{1,0:T(8,128)S(1)}, u32[]{:S(2)}, u32[]{:S(2)}) collective-permute-start(f32[8,2048]{1,0:T(8,128)S(1)} %get-tuple-element.35), channel_id=1, source_target_pairs={{0,8},{8,0},{16,24},{24,16},{1,9},{9,1},{17,25},{25,17},{2,10},{10... | collective-permute-start | bytes 196616 | tf_op jit(solution)/shard_map/ppermute | solution.py:84
  29.8 5.4 %collective-permute-start.8 = (f32[8,2048]{1,0:T(8,128)S(1)}, f32[8,2048]{1,0:T(8,128)S(1)}, u32[]{:S(2)}, u32[]{:S(2)}) collective-permute-start(f32[8,2048]{1,0:T(8,128)S(1)} %add.3.panel_ref), channel_id=1, source_target_pairs={{0,16},{8,24},{16,0},{24,8},{1,17},{9,25},{17,1},{25,9},{2,18},{10... | collective-permute-start | bytes 196616 | tf_op jit(solution)/shard_map/ppermute | solution.py:84
  44.2 5.6 %collective-permute-start.12 = (bf16[528,128]{1,0:T(8,128)(2,1)S(1)}, bf16[528,128]{1,0:T(8,128)(2,1)S(1)}, u32[]{:S(2)}, u32[]{:S(2)}) collective-permute-start(bf16[528,128]{1,0:T(8,128)(2,1)S(1)} %get-tuple-element.44), channel_id=1, source_target_pairs={{0,8},{8,0},{16,24},{24,16},{1,9},{9,1},{17,25},{25,17},{2,10},{10... | collective-permute-start | bytes 405512 | tf_op jit(solution)/shard_map/ppermute | solution.py:84
  45.9 10.6 %collective-permute-start.13 = (bf16[528,128]{1,0:T(8,128)(2,1)S(1)}, bf16[528,128]{1,0:T(8,128)(2,1)S(1)}, u32[]{:S(2)}, u32[]{:S(2)}) collective-permute-start(bf16[528,128]{1,0:T(8,128)(2,1)S(1)} %get-tuple-element.45), channel_id=1, source_target_pairs={{0,16},{8,24},{16,0},{24,8},{1,17},{9,25},{17,1},{25,9},{2,18},{10... | collective-permute-start | bytes 405512 | tf_op jit(solution)/shard_map/ppermute | solution.py:84
  48.5 8.0 %collective-permute-start.14 = (bf16[528,128]{1,0:T(8,128)(2,1)S(1)}, bf16[528,128]{1,0:T(8,128)(2,1)S(1)}, u32[]{:S(2)}, u32[]{:S(2)}) collective-permute-start(bf16[528,128]{1,0:T(8,128)(2,1)S(1)} %get-tuple-element.46), channel_id=1, source_target_pairs={{0,24},{8,16},{16,8},{24,0},{1,25},{9,17},{17,9},{25,1},{2,26},{10... | collective-permute-start | bytes 405512 | tf_op jit(solution)/shard_map/ppermute | solution.py:84
  56.9 5.9 %collective-permute-start.17 = (bf16[512,128]{1,0:T(8,128)(2,1)S(1)}, bf16[512,128]{1,0:T(8,128)(2,1)S(1)}, u32[]{:S(2)}, u32[]{:S(2)}) collective-permute-start(bf16[512,128]{1,0:T(8,128)(2,1)S(1)} %apply.1.refs_0_), channel_id=1, source_target_pairs={{0,6},{1,7},{2,4},{3,5},{4,2},{5,3},{6,0},{7,1},{8,14},{9,15},{10,... | collective-permute-start | bytes 393224 | tf_op jit(solution)/shard_map/ppermute | solution.py:84
  59.4 5.0 %collective-permute-start.16 = (bf16[512,128]{1,0:T(8,128)(2,1)S(1)}, bf16[512,128]{1,0:T(8,128)(2,1)S(1)}, u32[]{:S(2)}, u32[]{:S(2)}) collective-permute-start(bf16[512,128]{1,0:T(8,128)(2,1)S(1)} %apply.1.refs_0_), channel_id=1, source_target_pairs={{0,4},{1,5},{2,6},{3,7},{4,0},{5,1},{6,2},{7,3},{8,12},{9,13},{10,... | collective-permute-start | bytes 393224 | tf_op jit(solution)/shard_map/ppermute | solution.py:84
  59.9 5.0 %collective-permute-start.15 = (bf16[512,128]{1,0:T(8,128)(2,1)S(1)}, bf16[512,128]{1,0:T(8,128)(2,1)S(1)}, u32[]{:S(2)}, u32[]{:S(2)}) collective-permute-start(bf16[512,128]{1,0:T(8,128)(2,1)S(1)} %apply.1.refs_0_), channel_id=1, source_target_pairs={{0,2},{1,3},{2,0},{3,1},{4,6},{5,7},{6,4},{7,5},{8,10},{9,11},{10,... | collective-permute-start | bytes 393224 | tf_op jit(solution)/shard_map/ppermute | solution.py:84
  60.5 4.4 %collective-permute-start.18 = (bf16[512,128]{1,0:T(8,128)(2,1)S(1)}, bf16[512,128]{1,0:T(8,128)(2,1)S(1)}, u32[]{:S(2)}, u32[]{:S(2)}) collective-permute-start(bf16[512,128]{1,0:T(8,128)(2,1)S(1)} %apply.1.refs_0_), channel_id=1, source_target_pairs={{0,1},{1,0},{2,3},{3,2},{4,5},{5,4},{6,7},{7,6},{8,9},{9,8},{10,11... | collective-permute-start | bytes 393224 | tf_op jit(solution)/shard_map/ppermute | solution.py:84
  62.9 2.1 %collective-permute-start.21 = (bf16[512,128]{1,0:T(8,128)(2,1)S(1)}, bf16[512,128]{1,0:T(8,128)(2,1)S(1)}, u32[]{:S(2)}, u32[]{:S(2)}) collective-permute-start(bf16[512,128]{1,0:T(8,128)(2,1)S(1)} %collective-permute-done.17.refs_3_), channel_id=1, source_target_pairs={{0,1},{1,0},{2,3},{3,2},{4,5},{5,4},{6,7},{7,6},{8,9},{9,8},{10,11... | collective-permute-start | bytes 393224 | tf_op jit(solution)/shard_map/ppermute | solution.py:84
  64.4 1.3 %collective-permute-start.20 = (bf16[512,128]{1,0:T(8,128)(2,1)S(1)}, bf16[512,128]{1,0:T(8,128)(2,1)S(1)}, u32[]{:S(2)}, u32[]{:S(2)}) collective-permute-start(bf16[512,128]{1,0:T(8,128)(2,1)S(1)} %collective-permute-done.16.refs_2_), channel_id=1, source_target_pairs={{0,1},{1,0},{2,3},{3,2},{4,5},{5,4},{6,7},{7,6},{8,9},{9,8},{10,11... | collective-permute-start | bytes 393224 | tf_op jit(solution)/shard_map/ppermute | solution.py:84
  64.9 1.3 %collective-permute-start.19 = (bf16[512,128]{1,0:T(8,128)(2,1)S(1)}, bf16[512,128]{1,0:T(8,128)(2,1)S(1)}, u32[]{:S(2)}, u32[]{:S(2)}) collective-permute-start(bf16[512,128]{1,0:T(8,128)(2,1)S(1)} %collective-permute-done.15.refs_1_), channel_id=1, source_target_pairs={{0,1},{1,0},{2,3},{3,2},{4,5},{5,4},{6,7},{7,6},{8,9},{9,8},{10,11... | collective-permute-start | bytes 393224 | tf_op jit(solution)/shard_map/ppermute | solution.py:84
